TPU v7x, 32 devices: a whole 2x2x4 slice. The times are simulated.
32 devices in a mesh: ground: 16 (over z, x, core), pair: 2 (over y).
Axes of the slice: x: 2, y: 2, z: 4, core: 2. Of those that a mesh axis runs over, the one named last changes fastest.
Arguments:
- coregistered_sweeps: bfloat16 [2, 16, 512, 2, 512], P('pair', 'ground'), may hold values from -6 to 6
- shard_opening_height: int32 [1024], P('ground'), may hold values from 0 to 496
- shard_goal_patch: int32 [1024, 1], P('ground'), may hold values from 0 to 15; in each aligned block of 64 rows (0 to 63, 64 to 127, ...) at most 8 rows name the same one
- shard_patch_place: int32 [1024], P('ground'), may hold values from 0 to 31
Outputs:
- filtered: float32 [2, 1, 16, 2, 64, 64], P('pair', None, 'ground')
Inputs may be any that keep to these rules, and one draw needn't show every extreme that they name: `shard_goal_patch`: among the 64 pieces of the bursts of one ground index, at most 8 name the same ground tile.
All inputs are finite; a program needn't handle non-finite values.
Results may differ from a plain program's by a relative error of at most 0.0023.
Values may be sent and summed in bfloat16 or wider, within the bound.
A program may use at most 320 MiB of HBM per device.

v0:
```python
import math

import jax
import jax.numpy as jnp
from jax import lax
from jax.sharding import PartitionSpec as P

LOOK_ROWS = 4
LOOK_COLS = 16
SHARD_HEIGHT = 16
TILE_ROWS = 256
TILE_COLS = 1024
SWEEP_WIDTH = 512
PATCH_SHARD_LEVEL = 16
SLOTS = 32


def multilook(reference_tiles, secondary_tiles):
    first = reference_tiles.astype(jnp.float32)
    second = secondary_tiles.astype(jnp.float32)
    real_part = first[..., 0, :] * second[..., 0, :] + first[..., 1, :] * second[..., 1, :]
    imag_part = first[..., 1, :] * second[..., 0, :] - first[..., 0, :] * second[..., 1, :]
    joined = jnp.stack([real_part, imag_part], axis=-3)
    leading = joined.shape[:-2]
    row_count = joined.shape[-2]
    col_count = joined.shape[-1]
    boxes = joined.reshape(
        leading + (row_count // LOOK_ROWS, LOOK_ROWS, col_count // LOOK_COLS, LOOK_COLS)
    )
    return jnp.mean(boxes, axis=(-3, -1))


def on_left(matrix, field):
    return jnp.einsum("ij,...jk->...ik", matrix, field, precision=lax.Precision.HIGHEST)


def on_right(field, matrix):
    return jnp.einsum("...ij,jk->...ik", field, matrix, precision=lax.Precision.HIGHEST)


def goldstein(looked):
    length = looked.shape[-1]
    positions = jnp.arange(length, dtype=jnp.int32)
    phase = positions[:, None] * positions[None, :] % length
    angle = phase.astype(jnp.float32) * (2.0 * math.pi / length)
    cosine = jnp.cos(angle)
    sine = jnp.sin(angle)
    real_in = looked[..., 0, :, :]
    imag_in = looked[..., 1, :, :]
    half_real = on_left(cosine, real_in) + on_left(sine, imag_in)
    half_imag = on_left(cosine, imag_in) - on_left(sine, real_in)
    spec_real = on_right(half_real, cosine) + on_right(half_imag, sine)
    spec_imag = on_right(half_imag, cosine) - on_right(half_real, sine)
    weight = (spec_real * spec_real + spec_imag * spec_imag + 1e-06) ** 0.25
    weight = weight / jnp.mean(weight, axis=(-2, -1), keepdims=True)
    spec_real = spec_real * weight
    spec_imag = spec_imag * weight
    back_real = on_left(cosine, spec_real) - on_left(sine, spec_imag)
    back_imag = on_left(cosine, spec_imag) + on_left(sine, spec_real)
    out_real = on_right(back_real, cosine) - on_right(back_imag, sine)
    out_imag = on_right(back_imag, cosine) + on_right(back_real, sine)
    scale = 1.0 / (length * length)
    return jnp.stack([out_real * scale, out_imag * scale], axis=-3)


def partners_of(index, pair_width):
    order = jnp.arange(pair_width, dtype=jnp.int32)
    return order + (order >= index).astype(jnp.int32)


def local(coregistered_sweeps, shard_opening_height, shard_goal_patch, shard_patch_place):
    earth_patch_total_size = lax.axis_size("ground")
    pair_count = lax.axis_size("pair")
    piece_count = shard_opening_height.shape[0]
    place_allowance = max(
        2, (2 * piece_count + earth_patch_total_size - 1) // earth_patch_total_size
    )
    sweep_resident = coregistered_sweeps[0, 0]
    target = shard_goal_patch[:, 0]
    hits = (target[:, None] == jnp.arange(earth_patch_total_size, dtype=jnp.int32)[None, :]).astype(
        jnp.int32
    )
    earlier = jnp.cumsum(hits, axis=0) - hits
    rank = jnp.sum(earlier * hits, axis=1)
    position = target * place_allowance + rank
    matches = (
        position[None, :]
        == jnp.arange(earth_patch_total_size * place_allowance, dtype=jnp.int32)[:, None]
    ).astype(jnp.int32)
    tiles_filled = jnp.sum(matches, axis=1) > 0
    chosen = jnp.sum(matches * jnp.arange(piece_count, dtype=jnp.int32)[None, :], axis=1)
    sweep_height_offset = (
        shard_opening_height[chosen][:, None] + jnp.arange(SHARD_HEIGHT, dtype=jnp.int32)[None, :]
    )
    pieces_to_send = jnp.where(
        tiles_filled[:, None, None, None],
        sweep_resident[sweep_height_offset],
        jnp.zeros((), jnp.bfloat16),
    )
    labels = jnp.where(tiles_filled, shard_patch_place[chosen] + 1, 0).astype(jnp.bfloat16)
    received_pieces, arrived_labels = (
        lax.all_to_all(
            pieces_to_send.reshape(
                earth_patch_total_size, place_allowance, SHARD_HEIGHT, 2, SWEEP_WIDTH
            ),
            "ground",
            split_axis=0,
            concat_axis=0,
            tiled=True,
        ),
        lax.all_to_all(
            labels.reshape(earth_patch_total_size, place_allowance),
            "ground",
            split_axis=0,
            concat_axis=0,
            tiled=True,
        ),
    )
    pieces_flattened = received_pieces.reshape(
        earth_patch_total_size * place_allowance, SHARD_HEIGHT * 2 * SWEEP_WIDTH
    )
    slot_labels = (jnp.arange(SLOTS, dtype=jnp.int32) + 1).astype(jnp.bfloat16)
    selector = arrived_labels.reshape(-1)[None, :] == slot_labels[:, None]
    totals = jnp.dot(
        selector.astype(jnp.bfloat16), pieces_flattened, preferred_element_type=jnp.float32
    )
    counts = jnp.sum(selector.astype(jnp.float32), axis=1)
    smoothed_pixel_mean = (totals / jnp.maximum(counts, 1.0)[:, None]).astype(jnp.bfloat16)
    ground_tile = (
        smoothed_pixel_mean.reshape(PATCH_SHARD_LEVEL, 2, SHARD_HEIGHT, 2, SWEEP_WIDTH)
        .transpose(0, 2, 3, 1, 4)
        .reshape(TILE_ROWS, 2, TILE_COLS)
    )
    pair_width = pair_count - 1
    own_refs = partners_of(lax.axis_index("pair"), pair_width)
    piece = lax.all_gather(ground_tile[None], "pair", axis=0, tiled=True)
    looked_piece = multilook(piece, ground_tile[None])
    indices = jnp.arange(piece.shape[0], dtype=jnp.int32)
    selection = (own_refs[:, None] == indices[None, :]).astype(jnp.float32)
    looked = jnp.einsum("kn,nabc->kabc", selection, looked_piece, precision=lax.Precision.HIGHEST)
    return goldstein(looked)[None, :, None]


def solution(mesh):
    placed = (P("pair", "ground", None, None, None), P("ground"), P("ground", None), P("ground"))
    return jax.shard_map(
        local,
        mesh=mesh,
        in_specs=placed,
        out_specs=P("pair", None, "ground", None, None, None),
        check_vma=False,
    )
```

profile of v0, /device:TPU:3, one launch (start us, length us, event | category | flops | bytes accessed | tf_op | source)
XLA Modules:
  0.0 271.6 jit_solution(14282639509848993935)
XLA Ops:
  6.5 0.8 fusion.16
  7.4 0.1 reduce_window_sum.11
  7.4 0.8 select_reduce_fusion.1
  8.3 0.7 multiply_add_fusion.1
  9.0 0.1 convert_reduce_fusion
  9.1 1.6 gather_fusion
  10.7 0.7 convert_element_type.97
  11.4 6.7 %all-to-all-start = ((bf16[16,1,8]{2,1,0:T(2,128)(2,1)}), bf16[16,1,8]{2,1,0:T(2,128)(2,1)S(1)}, u32[]{:S(2)}, u32[]{:S(2)}) async-start(bf16[16,1,8]{2,1,0:T(2,128)(2,1)} %convert_element_type.97), calls=%async_computation | async-start | bytes 16384 | tf_op jit(solution)/shard_map/all_to_all | solution.py:111
  18.1 1.6 gather_fusion.1
  19.9 21.4 %gather_fusion.2 = bf16[2048,2,512]{2,1,0:T(2,128)(2,1)} fusion(bf16[512,2,512]{2,1,0:T(2,128)(2,1)S(1)} %bitcast.86, s32[2048]{0:T(1024)S(1)} %broadcast_clamp_fusion), kind=kCustom, calls=%fused_computation.2 | custom fusion | bytes 8396800 | tf_op jit(solution)/shard_map/gather | solution.py:97
  41.3 7.7 %broadcast_select_fusion = bf16[16,8,16,2,512]{4,3,2,1,0:T(2,128)(2,1)} fusion(bf16[16,8,16,2,512]{4,3,2,1,0:T(2,128)(2,1)} %bitcast.87, pred[16,8]{1,0:T(8,128)(4,1)S(1)} %gt.20), kind=kLoop, calls=%fused_computation.8 | loop fusion | flops 2097152 | bytes 8388736 | tf_op jit(solution)/shard_map/jit(_where)/select_n | solution.py:95
  49.0 6.0 %all-to-all-start.1 = ((bf16[16,8,16,2,512]{4,3,2,1,0:T(2,128)(2,1)}), bf16[16,8,16,2,512]{4,3,2,1,0:T(2,128)(2,1)}, u32[]{:S(2)}, u32[]{:S(2)}) async-start(bf16[16,8,16,2,512]{4,3,2,1,0:T(2,128)(2,1)} %broadcast_select_fusion), calls=%async_computation.1 | async-start | bytes 8388608 | tf_op jit(solution)/shard_map/all_to_all | solution.py:102
  55.0 0.2 all-gather.2.cloned.1.call-start
  55.3 0.1 eq.62
  55.4 0.2 fusion.21
  55.6 82.0 %all-to-all-done.1 = bf16[16,8,16,2,512]{4,3,2,1,0:T(2,128)(2,1)} async-done(((bf16[16,8,16,2,512]{4,3,2,1,0:T(2,128)(2,1)}), bf16[16,8,16,2,512]{4,3,2,1,0:T(2,128)(2,1)}, u32[]{:S(2)}, u32[]{:S(2)}) %all-to-all-start.1) | async-done | bytes 4194336 | tf_op jit(solution)/shard_map/all_to_all | solution.py:102
  137.6 7.8 %reshape.291 = bf16[128,16384]{1,0:T(8,128)(2,1)} reshape(bf16[16,8,16,2,512]{4,3,2,1,0:T(2,128)(2,1)} %all-to-all-done.1) | data formatting | bytes 8388608 | tf_op jit(solution)/shard_map/reshape | solution.py:119
  145.4 2.9 %fusion = bf16[32,16384]{1,0:T(8,128)(2,1)S(1)} fusion(bf16[128,16384]{1,0:T(8,128)(2,1)} %reshape.291, f32[32]{0:T(128)S(1)} %broadcast_maximum_fusion, bf16[128]{0:T(256)(128)(2,1)S(1)} %eq.62, bf16[32]{0:T(256)(128)(2,1)S(1)} %add_convert_fusion), kind=kOutput, calls=%fused_computation.5 | convolution fusion | flops 135270400 | bytes 5243328 | tf_op jit(solution)/shard_map/dot_general | solution.py:124
  148.4 0.8 reshape.292
  149.2 1.1 copy.19
  150.3 1.6 broadcast_in_dim_reshape.2
  151.8 1.4 fusion.126
  153.3 4.8 %mul.253 = f32[64,4,64,16]{3,2,1,0:T(8,128)} reshape(f32[1,256,1,1024]{3,1,2,0:T(8,128)S(1)} %get-tuple-element.11) | data formatting | bytes 2097152 | tf_op jit(solution)/shard_map/mul | solution.py:21
  158.1 4.8 %mul.256 = f32[64,4,64,16]{3,2,1,0:T(8,128)} reshape(f32[1,256,1,1024]{3,1,2,0:T(8,128)S(1)} %get-tuple-element.12) | data formatting | bytes 2097152 | tf_op jit(solution)/shard_map/mul | solution.py:21
  163.0 31.5 %all-gather.2.cloned.1.call-done = bf16[2,256,2,1024]{3,1,2,0:T(8,128)(2,1)} async-done(((bf16[1,256,2,1024]{3,1,2,0:T(8,128)(2,1)}), bf16[2,256,2,1024]{3,1,2,0:T(8,128)(2,1)}) %all-gather.2.cloned.1.call-update) | async-done | bytes 2097168 | tf_op jit(solution)/shard_map/all_gather | solution.py:136
  194.5 3.4 %fusion.125 = (f32[2,256,1,1024]{3,1,2,0:T(8,128)S(1)}, f32[2,256,1,1024]{3,1,2,0:T(8,128)}) fusion(bf16[2,256,2,1024]{3,1,2,0:T(8,128)(2,1)} %all-gather.2.cloned.1.call-done), kind=kLoop, calls=%fused_computation.149 | loop fusion | bytes 8388608 | tf_op jit(solution)/shard_map/slice | solution.py:21
  197.8 10.4 %squeeze.10 = f32[2,1,64,4,64,16]{5,4,3,2,0,1:T(8,128)} reshape(f32[2,256,1,1024]{3,1,2,0:T(8,128)} %get-tuple-element.10) | data formatting | bytes 4194304 | tf_op jit(solution)/shard_map/squeeze | solution.py:21
  208.2 9.0 %squeeze.11 = f32[2,1,64,4,64,16]{5,4,3,2,0,1:T(8,128)} reshape(f32[2,256,1,1024]{3,1,2,0:T(8,128)S(1)} %get-tuple-element.9) | data formatting | bytes 4194304 | tf_op jit(solution)/shard_map/squeeze | solution.py:21
  217.2 27.0 %multiply_add_fusion = (f32[2,1,64,4,64,16]{5,4,3,2,0,1:T(8,128)}, f32[2,1,64,4,64,16]{5,4,3,2,0,1:T(8,128)}) fusion(f32[2,1,64,4,64,16]{5,4,3,2,0,1:T(8,128)} %squeeze.11, f32[2,1,64,4,64,16]{5,4,3,2,0,1:T(8,128)} %squeeze.10, f32[64,4,64,16]{3,2,1,0:T(8,128)} %mul.256, f32[64,4,64,16]{3,2,1,0:T(8,128)} %mul.253), kind=kLoop, calls=%fused_computation.7 | loop fusion | flops 3145728 | bytes 10485760 | tf_op jit(solution)/shard_map/add | solution.py:21
  244.2 13.0 %maximum_reduce_fusion = f32[2,2,64,64]{3,2,0,1:T(8,128)S(1)} fusion(f32[2,1,64,4,64,16]{5,4,3,2,0,1:T(8,128)} %get-tuple-element.8, f32[2,1,64,4,64,16]{5,4,3,2,0,1:T(8,128)} %get-tuple-element.7), kind=kLoop, calls=%fused_computation.3 | loop fusion | flops 2080768 | bytes 4259840 | tf_op jit(solution)/shard_map/reduce_sum | solution.py:30
  257.3 0.4 fusion.9
  257.7 0.3 fusion.19
  258.0 0.3 fusion.18
  258.3 0.3 fusion.7
  258.7 0.3 fusion.8
  259.0 0.3 fusion.35
  259.3 0.3 fusion.32
  259.6 0.3 convolution_add_fusion.2
  259.9 0.9 fusion.51
  261.5 0.3 fusion.30
  261.9 0.3 fusion.26
  262.2 0.3 fusion.6
  262.5 0.3 fusion.28
  262.8 0.3 fusion.5
  263.2 0.3 fusion.24
  263.5 0.3 fusion.4
  263.8 0.3 fusion.2
  264.1 0.6 maximum_bitcast_fusion
  (18 shorter events, 0.4 us)
Async XLA Ops:
  6.5 13.4 %copy-start = (bf16[1,1,512,2,512]{4,3,2,1,0:T(2,128)(2,1)S(1)}, bf16[1,1,512,2,512]{4,3,2,1,0:T(2,128)(2,1)}, u32[]{:S(2)}) copy-start(bf16[1,1,512,2,512]{4,3,2,1,0:T(2,128)(2,1)} %param.4) | copy-start | bytes 3145732
  11.4 37.6 %all-to-all-start = ((bf16[16,1,8]{2,1,0:T(2,128)(2,1)}), bf16[16,1,8]{2,1,0:T(2,128)(2,1)S(1)}, u32[]{:S(2)}, u32[]{:S(2)}) async-start(bf16[16,1,8]{2,1,0:T(2,128)(2,1)} %convert_element_type.97), calls=%async_computation | async-start | bytes 16384 | tf_op jit(solution)/shard_map/all_to_all | solution.py:111
  49.0 88.6 %all-to-all-start.1 = ((bf16[16,8,16,2,512]{4,3,2,1,0:T(2,128)(2,1)}), bf16[16,8,16,2,512]{4,3,2,1,0:T(2,128)(2,1)}, u32[]{:S(2)}, u32[]{:S(2)}) async-start(bf16[16,8,16,2,512]{4,3,2,1,0:T(2,128)(2,1)} %broadcast_select_fusion), calls=%async_computation.1 | async-start | bytes 8388608 | tf_op jit(solution)/shard_map/all_to_all | solution.py:102
  55.0 139.4 %all-gather.2.cloned.1.call-start = ((), (), s32[]{:S(2)}) async-start(), calls=%async_computation.2 | async-start | bytes 3145728 | tf_op jit(solution)/shard_map/all_gather | solution.py:136
  244.2 20.5 %copy-start.1 = (bf16[1,1,512,2,512]{4,3,2,1,0:T(2,128)(2,1)S(1)}, bf16[1,1,512,2,512]{4,3,2,1,0:T(2,128)(2,1)}, u32[]{:S(2)}) copy-start(bf16[1,1,512,2,512]{4,3,2,1,0:T(2,128)(2,1)} %param.4) | copy-start | bytes 3145732
Sparse Core Ops, SparseCore 0:
  152.0 42.4 all-gather.1
where the time goes:
time: 274 us; the launch traced here: 272 us
  waiting for transfers between devices  114 us (42%)
  local copies, waits for them, and re-layouts  70.7 us (26%)
  other arithmetic  51.2 us (19%)
  between operations  14.3 us (5%)
  starting transfers between devices  12.9 us (5%)
  matrix products  8.98 us (3%)
    all_to_all x1, waiting for transfers between devices, local(): lax.all_to_all(pieces_to_send.reshape(earth_patch_total_size, place_allow...  82 us
    all_gather x1, waiting for transfers between devices, local(): piece = lax.all_gather(ground_tile[None], 'pair', axis=0, tiled=True)  31.5 us
    add x1, other arithmetic, multilook(): first[..., 0, :] * second[..., 0, :] + first[..., 1, :] * second[..., 1, :]  27 us
    gather x1, local copies, waits for them, and re-layouts, local(): sweep_resident[sweep_height_offset]  21.4 us
    reduce_sum x1, other arithmetic, multilook(): return jnp.mean(boxes, axis=(-3, -1))  13 us
    squeeze x1, local copies, waits for them, and re-layouts, multilook(): first[..., 0, :] * second[..., 0, :] + first[..., 1, :] * second[..., 1, :]  10.4 us
    squeeze x1, local copies, waits for them, and re-layouts, multilook(): first[..., 1, :] * second[..., 1, :]  8.98 us
    reshape x1, local copies, waits for them, and re-layouts, local(): received_pieces.reshape(earth_patch_total_size * place_allowance, SHARD_H...  7.8 us
  transfers between devices with their start and end apart: 3, of which 2 were waited for; matrix products, arithmetic and copies ran while one was open for 16% of the time, Pallas kernels for 0%

commit v1 on v0

--- a/solution.py
+++ b/solution.py
@@ -1,8 +1,12 @@
+import functools
 import math
 
 import jax
 import jax.numpy as jnp
+import numpy as np
 from jax import lax
+from jax.experimental import pallas as pl
+from jax.experimental.pallas import tpu as pltpu
 from jax.sharding import PartitionSpec as P
 
 LOOK_ROWS = 4
@@ -141,7 +145,7 @@
     return goldstein(looked)[None, :, None]
 
 
-def solution(mesh):
+def general(mesh):
     placed = (P("pair", "ground", None, None, None), P("ground"), P("ground", None), P("ground"))
     return jax.shard_map(
         local,
@@ -150,3 +154,320 @@
         out_specs=P("pair", None, "ground", None, None, None),
         check_vma=False,
     )
+
+
+CAP_VMEM = 48 * 1024 * 1024
+MESH = pl.DeviceIdType.MESH
+EXACT = lax.Precision.HIGHEST
+
+
+def table_kernel(allowance, opening, goal, place, starts, labels):
+    tile_count = starts.shape[0]
+    for tile in range(tile_count):
+        for slot in range(allowance):
+            starts[tile, slot] = 0
+            labels[tile, 0, slot] = 0
+
+    def clear(tile, carry):
+        labels[tile, 0, allowance] = 0
+        return carry
+
+    lax.fori_loop(0, tile_count, clear, 0)
+
+    def enter(piece, carry):
+        tile = goal[piece]
+        rank = labels[tile, 0, allowance]
+        starts[tile, rank] = opening[piece]
+        labels[tile, 0, rank] = place[piece] + 1
+        labels[tile, 0, allowance] = rank + 1
+        return carry
+
+    lax.fori_loop(0, opening.shape[0], enter, 0)
+
+
+def exchange_kernel(
+    tile_count, allowance, starts, labels, sweep, arrived, arrived_labels,
+    outgoing, send_sem, recv_sem, label_send, label_recv, own_sem,
+):
+    me = lax.axis_index("ground")
+    mine = lax.axis_index("pair")
+    half = SHARD_HEIGHT // 2
+    barrier = pltpu.get_barrier_semaphore()
+
+    def greet(step, carry):
+        pl.semaphore_signal(
+            barrier, inc=1,
+            device_id={"ground": lax.rem(me + step // 2, tile_count), "pair": lax.rem(mine + step, 2)},
+            device_id_type=MESH,
+        )
+        return carry
+
+    lax.fori_loop(1, 2 * tile_count, greet, 0)
+
+    def extract(tile):
+        def one(slot, carry):
+            top = starts[tile, slot]
+            outgoing[tile, 0, pl.ds(slot * half, half)] = sweep[pl.ds(top, half)]
+            outgoing[tile, 1, pl.ds(slot * half, half)] = sweep[pl.ds(top + half, half)]
+            return carry
+
+        lax.fori_loop(0, allowance, one, 0)
+
+    def parcel(tile, other, source, source_pair):
+        return pltpu.make_async_remote_copy(
+            src_ref=outgoing.at[tile, other],
+            dst_ref=arrived.at[source_pair, source],
+            send_sem=send_sem.at[tile, other],
+            recv_sem=recv_sem.at[source_pair, source],
+            device_id={"ground": tile, "pair": other},
+            device_id_type=MESH,
+        )
+
+    def tag(tile, source):
+        return pltpu.make_async_remote_copy(
+            src_ref=labels.at[tile],
+            dst_ref=arrived_labels.at[source],
+            send_sem=label_send.at[tile],
+            recv_sem=label_recv.at[source],
+            device_id={"ground": tile, "pair": mine},
+            device_id_type=MESH,
+        )
+
+    def target_of(step):
+        return lax.rem(me + step, tile_count)
+
+    first = target_of(tile_count // 2)
+    extract(first)
+    pl.semaphore_wait(barrier, 2 * tile_count - 1)
+
+    def send(tile):
+        parcel(tile, 1 - mine, me, mine).start()
+        parcel(tile, mine, me, mine).start()
+        tag(tile, me).start()
+
+    send(first)
+
+    def pairs(step, carry):
+        tile = target_of(tile_count // 2 + step)
+        extract(tile)
+        send(tile)
+        tile = target_of(tile_count // 2 - step)
+        extract(tile)
+        send(tile)
+        return carry
+
+    lax.fori_loop(1, tile_count // 2, pairs, 0)
+    extract(me)
+    parcel(me, 1 - mine, me, mine).start()
+    own = pltpu.make_async_copy(outgoing.at[me, mine], arrived.at[mine, me], own_sem.at[0])
+    own.start()
+    own_tag = pltpu.make_async_copy(labels.at[me], arrived_labels.at[me], own_sem.at[1])
+    own_tag.start()
+
+    def finish(step, carry):
+        tile = target_of(step)
+        parcel(tile, 1 - mine, tile, 1 - mine).wait_recv()
+        parcel(tile, mine, tile, mine).wait_recv()
+        tag(tile, tile).wait_recv()
+        parcel(tile, 1 - mine, me, mine).wait_send()
+        parcel(tile, mine, me, mine).wait_send()
+        tag(tile, me).wait_send()
+        return carry
+
+    lax.fori_loop(1, tile_count, finish, 0)
+    parcel(me, 1 - mine, me, 1 - mine).wait_recv()
+    parcel(me, 1 - mine, me, mine).wait_send()
+    own.wait()
+    own_tag.wait()
+
+
+def combine_kernel(allowance, labels, arrived, spread, mask, gather, looked, total, count, prods):
+    source = pl.program_id(0)
+    half = SHARD_HEIGHT // 2
+
+    @pl.when(source == 0)
+    def _():
+        total[...] = jnp.zeros_like(total)
+        for slot in range(SLOTS):
+            count[slot] = 0
+
+    for slot in range(allowance):
+        label = labels[source, 0, slot]
+
+        @pl.when(label > 0)
+        def _():
+            count[label - 1] = count[label - 1] + 1
+            for part in range(2):
+                total[part, label - 1] += arrived[part, 0, pl.ds(slot * half, half)].astype(jnp.float32)
+
+    @pl.when(source == pl.num_programs(0) - 1)
+    def _():
+        def one(level, carry):
+            for side in range(2):
+                slot = level * 2 + side
+                divisor = jnp.maximum(count[slot], 1).astype(jnp.float32)
+                first = (total[1, slot] / divisor).astype(jnp.bfloat16).astype(jnp.float32)
+                second = (total[0, slot] / divisor).astype(jnp.bfloat16).astype(jnp.float32)
+                same = first * second
+                cross = first * jnp.concatenate([second[:, 4:], second[:, :4]], axis=1)
+                for box in range(2):
+                    rows = slice(box * LOOK_ROWS, (box + 1) * LOOK_ROWS)
+                    at = pl.ds(pl.multiple_of((level * 2 + box) * 8, 8), 8)
+                    prods[side, 0, at, :] = jnp.sum(same[rows], axis=0)
+                    prods[side, 1, at, :] = jnp.sum(cross[rows], axis=0)
+            return carry
+
+        lax.fori_loop(0, PATCH_SHARD_LEVEL, one, 0)
+        pooled = jnp.zeros(mask.shape[1:], jnp.float32)
+        for side in range(2):
+            wide = jnp.dot(prods[side, 0], spread[0], precision=EXACT, preferred_element_type=jnp.float32)
+            wide += jnp.dot(prods[side, 1], spread[1], precision=EXACT, preferred_element_type=jnp.float32)
+            pooled += wide * mask[side]
+        looked[...] = jnp.dot(gather[...], pooled, precision=EXACT, preferred_element_type=jnp.float32)
+
+
+def filter_kernel(looked, place, left, right, right_back, out, other, send_sem, recv_sem):
+    mine = lax.axis_index("pair")
+    barrier = pltpu.get_barrier_semaphore()
+    pl.semaphore_signal(barrier, inc=1, device_id={"pair": 1 - mine}, device_id_type=MESH)
+    pl.semaphore_wait(barrier, 1)
+    copy = pltpu.make_async_remote_copy(
+        src_ref=looked, dst_ref=other, send_sem=send_sem, recv_sem=recv_sem,
+        device_id={"pair": 1 - mine}, device_id_type=MESH,
+    )
+    copy.start()
+
+    def dot(a, b):
+        return jnp.dot(a, b, precision=EXACT, preferred_element_type=jnp.float32)
+
+    length = left.shape[1]
+    lane = lax.broadcasted_iota(jnp.int32, (length, 2 * length), 1)
+    turn = jnp.where(lane < length, 1.0, -1.0)
+    flip = jnp.where(lane < length, 1.0, 1.0 - 2.0 * mine.astype(jnp.float32))
+    own = dot(place[mine], looked[...])
+    copy.wait()
+    field = (own + dot(place[1 - mine], other[...])) * flip
+    both = dot(left[...], field)
+    spectrum = both[:length] + turn * pltpu.roll(both[length:], length, 1)
+    spectrum = dot(spectrum, right[...])
+    power = spectrum * spectrum
+    power = power + pltpu.roll(power, length, 1)
+    weight = jnp.sqrt(jnp.sqrt(power + 1e-06))
+    mean = jnp.sum(weight) * (1.0 / (2 * length * length))
+    spectrum = spectrum * (weight / mean)
+    both = dot(left[...], spectrum)
+    back = both[:length] - turn * pltpu.roll(both[length:], length, 1)
+    back = dot(back, right_back[...]) * (1.0 / (length * length))
+    out[0] = back[:, :length]
+    out[1] = back[:, length:]
+
+
+def constants():
+    lane = np.arange(128)
+    column = np.arange(64)
+    pick = (lane[:, None] // LOOK_COLS == column[None, :] % 8).astype(np.float32)
+    nil = np.zeros_like(pick)
+    spread = np.stack([np.concatenate([pick, nil], 1), np.concatenate([nil, pick], 1)])
+    sub = np.arange(256) % 8
+    masks = []
+    for side in range(2):
+        hit = (column[None, :] // 8 == side * 4 + sub[:, None] % 4).astype(np.float32)
+        sign = np.where(sub[:, None] < 4, -1.0, 1.0).astype(np.float32)
+        masks.append(np.concatenate([hit, hit * sign], 1))
+    mask = np.stack(masks)
+    gather = (np.arange(32)[:, None] == np.arange(256)[None, :] // 8).astype(np.float32)
+    gather = gather / (LOOK_ROWS * LOOK_COLS)
+    row = np.arange(32)
+    place = np.zeros((2, 64, 32), np.float32)
+    for pair in range(2):
+        place[pair, 4 * (row // 2) + 2 * pair + row % 2, row] = 1.0
+    angle = (column[:, None] * column[None, :] % 64) * (2.0 * math.pi / 64)
+    cosine, sine = np.cos(angle), np.sin(angle)
+    left = np.concatenate([cosine, sine], 0)
+    right = np.block([[cosine, -sine], [sine, cosine]])
+    right_back = np.block([[cosine, sine], [-sine, cosine]])
+    return (spread, mask, gather), tuple(x.astype(np.float32) for x in (place, left, right, right_back))
+
+
+def local_pair(coregistered_sweeps, shard_opening_height, shard_goal_patch, shard_patch_place):
+    tile_count = lax.axis_size("ground")
+    piece_count = shard_opening_height.shape[0]
+    allowance = max(2, (2 * piece_count + tile_count - 1) // tile_count)
+    half = SHARD_HEIGHT // 2
+    pool, transforms = constants()
+    smem = pl.BlockSpec(memory_space=pltpu.SMEM)
+    vmem = pl.BlockSpec(memory_space=pltpu.VMEM)
+    anyplace = pl.BlockSpec(memory_space=pl.ANY)
+    starts, labels = pl.pallas_call(
+        functools.partial(table_kernel, allowance),
+        out_shape=(
+            jax.ShapeDtypeStruct((tile_count, allowance), jnp.int32),
+            jax.ShapeDtypeStruct((tile_count, 1, 128), jnp.int32),
+        ),
+        in_specs=[smem] * 3,
+        out_specs=(smem, smem),
+    )(shard_opening_height, shard_goal_patch[:, 0], shard_patch_place)
+    sweep = coregistered_sweeps[0, 0].reshape(-1, 8, 128)
+    arrived, arrived_labels = pl.pallas_call(
+        functools.partial(exchange_kernel, tile_count, allowance),
+        out_shape=(
+            jax.ShapeDtypeStruct((2, tile_count, allowance * half, 8, 128), jnp.bfloat16),
+            jax.ShapeDtypeStruct((tile_count, 1, 128), jnp.int32),
+        ),
+        in_specs=[smem, vmem, vmem],
+        out_specs=(anyplace, vmem),
+        scratch_shapes=[
+            pltpu.VMEM((tile_count, 2, allowance * half, 8, 128), jnp.bfloat16),
+            pltpu.SemaphoreType.DMA((tile_count, 2)),
+            pltpu.SemaphoreType.DMA((2, tile_count)),
+            pltpu.SemaphoreType.DMA((tile_count,)),
+            pltpu.SemaphoreType.DMA((tile_count,)),
+            pltpu.SemaphoreType.DMA((2,)),
+        ],
+        compiler_params=pltpu.CompilerParams(
+            collective_id=0, has_side_effects=True, vmem_limit_bytes=CAP_VMEM
+        ),
+    )(starts, labels, sweep)
+    looked = pl.pallas_call(
+        functools.partial(combine_kernel, allowance),
+        grid=(tile_count,),
+        out_shape=jax.ShapeDtypeStruct((32, 128), jnp.float32),
+        in_specs=[
+            smem,
+            pl.BlockSpec((2, 1, allowance * half, 8, 128), lambda i: (0, i, 0, 0, 0)),
+            vmem, vmem, vmem,
+        ],
+        out_specs=vmem,
+        scratch_shapes=[
+            pltpu.VMEM((2, SLOTS, half, 8, 128), jnp.float32),
+            pltpu.SMEM((SLOTS,), jnp.int32),
+            pltpu.VMEM((2, 2, 256, 128), jnp.float32),
+        ],
+        compiler_params=pltpu.CompilerParams(vmem_limit_bytes=CAP_VMEM),
+    )(arrived_labels, arrived, *pool)
+    filtered = pl.pallas_call(
+        filter_kernel,
+        out_shape=jax.ShapeDtypeStruct((2, 64, 64), jnp.float32),
+        in_specs=[vmem] * 5,
+        out_specs=vmem,
+        scratch_shapes=[
+            pltpu.VMEM((32, 128), jnp.float32),
+            pltpu.SemaphoreType.DMA,
+            pltpu.SemaphoreType.DMA,
+        ],
+        compiler_params=pltpu.CompilerParams(collective_id=1, has_side_effects=True),
+    )(looked, *transforms)
+    return filtered[None, None, None]
+
+
+def solution(mesh):
+    if mesh.shape["pair"] != 2:
+        return general(mesh)
+    placed = (P("pair", "ground", None, None, None), P("ground"), P("ground", None), P("ground"))
+    return jax.shard_map(
+        local_pair,
+        mesh=mesh,
+        in_specs=placed,
+        out_specs=P("pair", None, "ground", None, None, None),
+        check_vma=False,
+    )

time: 274 us -> 124 us (0.45)
  the two profiles are of different devices: /device:TPU:3 before, /device:TPU:16 now
where the time goes in v1:
time: 124 us; the launch traced here: 123 us
  Pallas kernels  116 us (94%)
  local copies, waits for them, and re-layouts  7.81 us (6%)
    pallas_call x1, Pallas kernels, local_pair(): pl.pallas_call(functools.partial(exchange_kernel, tile_count, allowance),...  102 us
    pallas_call x1, Pallas kernels, local_pair(): pl.pallas_call(filter_kernel, out_shape=jax.ShapeDtypeStruct((2, 64, 64),...  6.79 us
    unnamed x13, local copies, waits for them, and re-layouts  6.07 us
    pallas_call x1, Pallas kernels, local_pair(): pl.pallas_call(functools.partial(combine_kernel, allowance), grid=(tile_c...  4.48 us
    pallas_call x1, Pallas kernels, local_pair(): pl.pallas_call(functools.partial(table_kernel, allowance), out_shape=(jax...  2.5 us

profile of v1, /device:TPU:16, one launch (start us, length us, event | category | flops | bytes accessed | tf_op | source)
XLA Modules:
  0.0 123.4 jit_solution(4304792612429667307)
XLA Ops:
  0.0 2.5 %shard_map.109 = (s32[16,8]{1,0:T(8,128)}, s32[16,1,128]{2,1,0:T(1,128)}) custom-call(s32[64]{0:T(128)} %opening.1, s32[64]{0:T(128)} %bitcast.3, s32[64]{0:T(128)} %place.2), custom_call_target="tpu_custom_call" | custom-call | tf_op jit(solution)/shard_map/pallas_call | solution.py:401
  2.5 1.7 %reshape_squeeze.3.sweep = bf16[512,8,128]{2,1,0:T(8,128)(2,1)S(1)} reshape(bf16[1,1,512,2,512]{4,3,2,1,0:T(2,128)(2,1)} %param.11) | data formatting | bytes 2097152 | tf_op jit(solution)/shard_map/reshape;squeeze | solution.py:410
  4.3 0.0 copy-start.4
  4.3 0.7 copy-done.4
  5.0 0.0 copy-start.5
  5.0 0.7 copy-done.5
  5.7 101.8 %shard_map.110 = (bf16[2,16,64,8,128]{4,3,2,1,0:T(8,128)(2,1)S(1)}, s32[16,1,128]{2,1,0:T(1,128)S(1)}) custom-call(s32[16,8]{1,0:T(8,128)S(1)} %copy-done.4, s32[16,1,128]{2,1,0:T(1,128)S(1)} %copy-done.5, bf16[512,8,128]{2,1,0:T(8,128)(2,1)S(1)} %reshape_squeeze.3.sweep), custom_call_target="tpu_custom_call" | custom-call | tf_op jit(solution)/shard_map/pallas_call | solution.py:411
  107.4 0.0 copy-start
  107.4 0.9 copy-done
  108.4 0.0 copy-start.1
  108.4 0.9 copy-done.1
  109.3 0.0 copy-start.3
  109.3 0.8 copy-done.3
  110.0 4.5 %shard_map.111.looked = f32[32,128]{1,0:T(8,128)S(1)} custom-call(s32[16,1,128]{2,1,0:T(1,128)S(1)} %get-tuple-element.11.labels, bf16[2,16,64,8,128]{4,3,2,1,0:T(8,128)(2,1)S(1)} %get-tuple-element.12.arrived, f32[2,128,128]{2,1,0:T(8,128)S(1)} %copy-done.1, f32[2,256,128]{2,1,0:T(8,128)S(1)} %copy-done, f32[32,256]{1,0:T(8,128)S(1)} %copy-done.3), custom_call_target="tpu_custom_call" | custom-call | tf_op jit(solution)/shard_map/pallas_call | solution.py:431
  114.5 0.0 copy-start.2
  114.5 0.6 copy-done.2
  115.1 6.8 %shard_map.112 = f32[2,64,64]{2,1,0:T(8,128)} custom-call(f32[32,128]{1,0:T(8,128)} %copy-done.2, f32[2,64,32]{2,1,0:T(8,128)} %constant.17.clone.place, f32[128,64]{1,0:T(8,128)} %constant.18.clone.left, f32[128,128]{1,0:T(8,128)} %constant.19.clone.right, f32[128,128]{1,0:T(8,128)} %constant.20.clone.right_back), custom_call_target="tpu_custom_call" | custom-call | tf_op jit(solution)/shard_map/pallas_call | solution.py:448
  121.9 1.5 %copy.13 = f32[1,1,1,2,64,64]{5,4,3,2,1,0:T(8,128)} copy(f32[1,1,1,2,64,64]{5,4,3,2,1,0:T(8,128)} %bitcast.2) | data formatting | bytes 65536
Async XLA Ops:
  4.3 0.7 copy-start.4
  5.0 0.7 copy-start.5
  107.4 1.0 copy-start
  108.4 0.9 copy-start.1
  109.3 0.8 copy-start.3
  114.5 0.6 copy-start.2

commit v2 on v1

--- a/solution.py
+++ b/solution.py
@@ -156,19 +156,19 @@
     )
 
 
-CAP_VMEM = 48 * 1024 * 1024
+CHUNKS = 2
 MESH = pl.DeviceIdType.MESH
 EXACT = lax.Precision.HIGHEST
 
 
 def table_kernel(allowance, opening, goal, place, starts, labels):
     tile_count = starts.shape[0]
-    for tile in range(tile_count):
+
+    def clear(tile, carry):
         for slot in range(allowance):
             starts[tile, slot] = 0
             labels[tile, 0, slot] = 0
-
-    def clear(tile, carry):
+            labels[tile, 0, 2 * allowance + slot] = 0
         labels[tile, 0, allowance] = 0
         return carry
 
@@ -179,6 +179,7 @@
         rank = labels[tile, 0, allowance]
         starts[tile, rank] = opening[piece]
         labels[tile, 0, rank] = place[piece] + 1
+        labels[tile, 0, 2 * allowance + rank] = opening[piece]
         labels[tile, 0, allowance] = rank + 1
         return carry
 
@@ -186,12 +187,22 @@
 
 
 def exchange_kernel(
-    tile_count, allowance, starts, labels, sweep, arrived, arrived_labels,
+    allowance, starts, labels, sweep, arrived, relayed, arrived_labels,
     outgoing, send_sem, recv_sem, label_send, label_recv, own_sem,
+    burst_send, relay_send, relay_recv,
 ):
     me = lax.axis_index("ground")
     mine = lax.axis_index("pair")
-    half = SHARD_HEIGHT // 2
+    tile_count = 16
+    level = me // 4
+    line = lax.rem(me, 4)
+    across = lax.rem(line + 2, 4)
+    beside = line + 1 - 2 * lax.rem(line, 2)
+    across_beside = lax.rem(beside + 2, 4)
+    inner = jnp.logical_or(level == 1, level == 2)
+    right = level // 2
+    outward = 3 * right
+    far = 2 - right
     barrier = pltpu.get_barrier_semaphore()
 
     def greet(step, carry):
@@ -207,8 +218,10 @@
     def extract(tile):
         def one(slot, carry):
             top = starts[tile, slot]
-            outgoing[tile, 0, pl.ds(slot * half, half)] = sweep[pl.ds(top, half)]
-            outgoing[tile, 1, pl.ds(slot * half, half)] = sweep[pl.ds(top + half, half)]
+            for part in range(2):
+                outgoing[tile, part, pl.ds(slot * SHARD_HEIGHT, SHARD_HEIGHT)] = sweep[
+                    part, pl.ds(top, SHARD_HEIGHT)
+                ]
             return carry
 
         lax.fori_loop(0, allowance, one, 0)
@@ -233,27 +246,58 @@
             device_id_type=MESH,
         )
 
+    span = sweep.shape[1] // CHUNKS
+
+    def burst(part, chunk):
+        rows = pl.ds(chunk * span, span)
+        return pltpu.make_async_remote_copy(
+            src_ref=sweep.at[part, rows],
+            dst_ref=relayed.at[line, mine, rows],
+            send_sem=burst_send.at[part, chunk],
+            recv_sem=relay_recv.at[line, mine, chunk],
+            device_id={"ground": far * 4 + line, "pair": part},
+            device_id_type=MESH,
+        )
+
+    def relay(kind, which, target, pair, chunk):
+        rows = pl.ds(chunk * span, span)
+        return pltpu.make_async_remote_copy(
+            src_ref=relayed.at[which, pair, rows],
+            dst_ref=relayed.at[which, pair, rows],
+            send_sem=relay_send.at[kind, pair, chunk],
+            recv_sem=relay_recv.at[which, pair, chunk],
+            device_id={"ground": target, "pair": mine},
+            device_id_type=MESH,
+        )
+
     def target_of(step):
         return lax.rem(me + step, tile_count)
 
-    first = target_of(tile_count // 2)
-    extract(first)
+    def takes(tile):
+        return jnp.logical_or(jnp.logical_not(inner), tile // 8 == right)
+
+    def send(tile):
+        tag(tile, me).start()
+
+        @pl.when(takes(tile))
+        def _():
+            extract(tile)
+            parcel(tile, 1 - mine, me, mine).start()
+            parcel(tile, mine, me, mine).start()
+
     pl.semaphore_wait(barrier, 2 * tile_count - 1)
 
-    def send(tile):
-        parcel(tile, 1 - mine, me, mine).start()
-        parcel(tile, mine, me, mine).start()
-        tag(tile, me).start()
-
-    send(first)
+    @pl.when(inner)
+    def _():
+        for chunk in range(CHUNKS):
+            for part in range(2):
+                burst(part, chunk).start()
+
+    send(target_of(tile_count // 2))
 
     def pairs(step, carry):
-        tile = target_of(tile_count // 2 + step)
-        extract(tile)
-        send(tile)
-        tile = target_of(tile_count // 2 - step)
-        extract(tile)
-        send(tile)
+        send(target_of(tile_count // 2 + step))
+        send(target_of(tile_count // 2 - step))
         return carry
 
     lax.fori_loop(1, tile_count // 2, pairs, 0)
@@ -264,14 +308,54 @@
     own_tag = pltpu.make_async_copy(labels.at[me], arrived_labels.at[me], own_sem.at[1])
     own_tag.start()
 
+    base = level * 4
+    order = [(pair, chunk) for chunk in range(CHUNKS) for pair in range(2)]
+
+    def second(pair, chunk):
+        relay(1, across, base + across, pair, chunk).wait_recv()
+        relay(3, across, base + beside, pair, chunk).start()
+
+    for spot, (pair, chunk) in enumerate(order):
+        relay(0, line, base + across, pair, chunk).wait_recv()
+
+        @pl.when(inner)
+        def _():
+            relay(0, line, outward * 4 + line, pair, chunk).start()
+
+        relay(1, line, base + across, pair, chunk).start()
+        relay(2, line, base + beside, pair, chunk).start()
+        if spot:
+            second(*order[spot - 1])
+    second(*order[-1])
+
+    for pair, chunk in order:
+        relay(2, beside, base + beside, pair, chunk).wait_recv()
+        relay(3, across_beside, base + beside, pair, chunk).wait_recv()
+
+        @pl.when(inner)
+        def _():
+            relay(0, line, outward * 4 + line, pair, chunk).wait_send()
+            burst(pair, chunk).wait_send()
+
+        relay(1, line, base + across, pair, chunk).wait_send()
+        relay(2, line, base + beside, pair, chunk).wait_send()
+        relay(3, across, base + beside, pair, chunk).wait_send()
+
     def finish(step, carry):
         tile = target_of(step)
-        parcel(tile, 1 - mine, tile, 1 - mine).wait_recv()
-        parcel(tile, mine, tile, mine).wait_recv()
         tag(tile, tile).wait_recv()
-        parcel(tile, 1 - mine, me, mine).wait_send()
-        parcel(tile, mine, me, mine).wait_send()
         tag(tile, me).wait_send()
+
+        @pl.when(tile // 4 != far)
+        def _():
+            parcel(tile, 1 - mine, tile, 1 - mine).wait_recv()
+            parcel(tile, mine, tile, mine).wait_recv()
+
+        @pl.when(takes(tile))
+        def _():
+            parcel(tile, 1 - mine, me, mine).wait_send()
+            parcel(tile, mine, me, mine).wait_send()
+
         return carry
 
     lax.fori_loop(1, tile_count, finish, 0)
@@ -281,52 +365,69 @@
     own_tag.wait()
 
 
-def combine_kernel(allowance, labels, arrived, spread, mask, gather, looked, total, count, prods):
-    source = pl.program_id(0)
-    half = SHARD_HEIGHT // 2
-
-    @pl.when(source == 0)
-    def _():
-        total[...] = jnp.zeros_like(total)
-        for slot in range(SLOTS):
-            count[slot] = 0
-
-    for slot in range(allowance):
-        label = labels[source, 0, slot]
-
-        @pl.when(label > 0)
-        def _():
-            count[label - 1] = count[label - 1] + 1
-            for part in range(2):
-                total[part, label - 1] += arrived[part, 0, pl.ds(slot * half, half)].astype(jnp.float32)
-
-    @pl.when(source == pl.num_programs(0) - 1)
-    def _():
-        def one(level, carry):
-            for side in range(2):
-                slot = level * 2 + side
-                divisor = jnp.maximum(count[slot], 1).astype(jnp.float32)
-                first = (total[1, slot] / divisor).astype(jnp.bfloat16).astype(jnp.float32)
-                second = (total[0, slot] / divisor).astype(jnp.bfloat16).astype(jnp.float32)
-                same = first * second
-                cross = first * jnp.concatenate([second[:, 4:], second[:, :4]], axis=1)
-                for box in range(2):
-                    rows = slice(box * LOOK_ROWS, (box + 1) * LOOK_ROWS)
-                    at = pl.ds(pl.multiple_of((level * 2 + box) * 8, 8), 8)
-                    prods[side, 0, at, :] = jnp.sum(same[rows], axis=0)
-                    prods[side, 1, at, :] = jnp.sum(cross[rows], axis=0)
-            return carry
-
-        lax.fori_loop(0, PATCH_SHARD_LEVEL, one, 0)
-        pooled = jnp.zeros(mask.shape[1:], jnp.float32)
+def combine_kernel(allowance, where, labels, arrived, relayed, spread, gather, looked, total, count, prods):
+    far = where[0]
+    mine = where[1]
+    total[...] = jnp.zeros_like(total)
+    for slot in range(SLOTS):
+        count[slot] = 0
+
+    def add(source, load):
+        for slot in range(allowance):
+            label = labels[source, 0, slot]
+
+            @pl.when(label > 0)
+            def _():
+                count[label - 1] = count[label - 1] + 1
+                for part in range(2):
+                    total[part, label - 1] += load(part, slot).astype(jnp.float32)
+
+    def one_source(source, carry):
+        @pl.when(source // 4 != far)
+        def _():
+            add(source, lambda part, slot: arrived[part, source, pl.ds(slot * SHARD_HEIGHT, SHARD_HEIGHT)])
+
+        @pl.when(source // 4 == far)
+        def _():
+            def load(part, slot):
+                top = labels[source, 0, 2 * allowance + slot]
+                return relayed[lax.rem(source, 4), part, pl.ds(top, SHARD_HEIGHT)]
+
+            add(source, load)
+
+        return carry
+
+    lax.fori_loop(0, arrived.shape[1], one_source, 0)
+
+    def one(level, carry):
         for side in range(2):
-            wide = jnp.dot(prods[side, 0], spread[0], precision=EXACT, preferred_element_type=jnp.float32)
-            wide += jnp.dot(prods[side, 1], spread[1], precision=EXACT, preferred_element_type=jnp.float32)
-            pooled += wide * mask[side]
-        looked[...] = jnp.dot(gather[...], pooled, precision=EXACT, preferred_element_type=jnp.float32)
-
-
-def filter_kernel(looked, place, left, right, right_back, out, other, send_sem, recv_sem):
+            slot = level * 2 + side
+            divisor = jnp.maximum(count[slot], 1).astype(jnp.float32)
+            first = (total[1, slot] / divisor).astype(jnp.bfloat16).astype(jnp.float32)
+            second = (total[0, slot] / divisor).astype(jnp.bfloat16).astype(jnp.float32)
+            same = first * second
+            cross = first * jnp.concatenate([second[:, 2:], second[:, :2]], axis=1)
+            for kind, value in ((0, same), (1, cross)):
+                boxes = [jnp.sum(value[box * LOOK_ROWS : (box + 1) * LOOK_ROWS], axis=0) for box in range(4)]
+                for two in range(2):
+                    at = pl.ds(pl.multiple_of((level * 2 + two) * 8, 8), 8)
+                    prods[side, kind, at, :] = jnp.concatenate(boxes[2 * two : 2 * two + 2], axis=0)
+        return carry
+
+    lax.fori_loop(0, PATCH_SHARD_LEVEL, one, 0)
+    sub = lax.rem(lax.broadcasted_iota(jnp.int32, (256, 128), 0), 4)
+    lane = lax.broadcasted_iota(jnp.int32, (256, 128), 1)
+    column = lax.rem(lane, 64)
+    sign = jnp.where(jnp.logical_and(lane >= 64, sub < 2), -1.0, 1.0)
+    pooled = jnp.zeros((256, 128), jnp.float32)
+    for side in range(2):
+        wide = jnp.dot(prods[side, 0], spread[0], precision=EXACT, preferred_element_type=jnp.float32)
+        wide += jnp.dot(prods[side, 1], spread[1], precision=EXACT, preferred_element_type=jnp.float32)
+        pooled += jnp.where(column // 8 == side * 4 + mine * 2 + lax.rem(sub, 2), wide * sign, 0.0)
+    looked[...] = jnp.dot(gather[...], pooled, precision=EXACT, preferred_element_type=jnp.float32)
+
+
+def filter_kernel(looked, left, right, right_back, out, other, send_sem, recv_sem):
     mine = lax.axis_index("pair")
     barrier = pltpu.get_barrier_semaphore()
     pl.semaphore_signal(barrier, inc=1, device_id={"pair": 1 - mine}, device_id_type=MESH)
@@ -344,9 +445,8 @@
     lane = lax.broadcasted_iota(jnp.int32, (length, 2 * length), 1)
     turn = jnp.where(lane < length, 1.0, -1.0)
     flip = jnp.where(lane < length, 1.0, 1.0 - 2.0 * mine.astype(jnp.float32))
-    own = dot(place[mine], looked[...])
     copy.wait()
-    field = (own + dot(place[1 - mine], other[...])) * flip
+    field = (looked[...] + other[...]) * flip
     both = dot(left[...], field)
     spectrum = both[:length] + turn * pltpu.roll(both[length:], length, 1)
     spectrum = dot(spectrum, right[...])
@@ -368,32 +468,20 @@
     pick = (lane[:, None] // LOOK_COLS == column[None, :] % 8).astype(np.float32)
     nil = np.zeros_like(pick)
     spread = np.stack([np.concatenate([pick, nil], 1), np.concatenate([nil, pick], 1)])
-    sub = np.arange(256) % 8
-    masks = []
-    for side in range(2):
-        hit = (column[None, :] // 8 == side * 4 + sub[:, None] % 4).astype(np.float32)
-        sign = np.where(sub[:, None] < 4, -1.0, 1.0).astype(np.float32)
-        masks.append(np.concatenate([hit, hit * sign], 1))
-    mask = np.stack(masks)
-    gather = (np.arange(32)[:, None] == np.arange(256)[None, :] // 8).astype(np.float32)
+    gather = (column[:, None] == np.arange(256)[None, :] // 4).astype(np.float32)
     gather = gather / (LOOK_ROWS * LOOK_COLS)
-    row = np.arange(32)
-    place = np.zeros((2, 64, 32), np.float32)
-    for pair in range(2):
-        place[pair, 4 * (row // 2) + 2 * pair + row % 2, row] = 1.0
     angle = (column[:, None] * column[None, :] % 64) * (2.0 * math.pi / 64)
     cosine, sine = np.cos(angle), np.sin(angle)
     left = np.concatenate([cosine, sine], 0)
     right = np.block([[cosine, -sine], [sine, cosine]])
     right_back = np.block([[cosine, sine], [-sine, cosine]])
-    return (spread, mask, gather), tuple(x.astype(np.float32) for x in (place, left, right, right_back))
+    return (spread, gather), tuple(x.astype(np.float32) for x in (left, right, right_back))
 
 
 def local_pair(coregistered_sweeps, shard_opening_height, shard_goal_patch, shard_patch_place):
     tile_count = lax.axis_size("ground")
     piece_count = shard_opening_height.shape[0]
     allowance = max(2, (2 * piece_count + tile_count - 1) // tile_count)
-    half = SHARD_HEIGHT // 2
     pool, transforms = constants()
     smem = pl.BlockSpec(memory_space=pltpu.SMEM)
     vmem = pl.BlockSpec(memory_space=pltpu.VMEM)
@@ -407,51 +495,59 @@
         in_specs=[smem] * 3,
         out_specs=(smem, smem),
     )(shard_opening_height, shard_goal_patch[:, 0], shard_patch_place)
-    sweep = coregistered_sweeps[0, 0].reshape(-1, 8, 128)
-    arrived, arrived_labels = pl.pallas_call(
-        functools.partial(exchange_kernel, tile_count, allowance),
+    height = coregistered_sweeps.shape[2]
+    sweep = (
+        coregistered_sweeps[0, 0]
+        .reshape(height, 2, 2, 2, 128)
+        .transpose(2, 0, 1, 3, 4)
+        .reshape(2, height, 4, 128)
+    )
+    depth = allowance * SHARD_HEIGHT
+    arrived, relayed, arrived_labels = pl.pallas_call(
+        functools.partial(exchange_kernel, allowance),
         out_shape=(
-            jax.ShapeDtypeStruct((2, tile_count, allowance * half, 8, 128), jnp.bfloat16),
+            jax.ShapeDtypeStruct((2, tile_count, depth, 4, 128), jnp.bfloat16),
+            jax.ShapeDtypeStruct((4, 2, height, 4, 128), jnp.bfloat16),
             jax.ShapeDtypeStruct((tile_count, 1, 128), jnp.int32),
         ),
         in_specs=[smem, vmem, vmem],
-        out_specs=(anyplace, vmem),
+        out_specs=(anyplace, anyplace, vmem),
         scratch_shapes=[
-            pltpu.VMEM((tile_count, 2, allowance * half, 8, 128), jnp.bfloat16),
+            pltpu.VMEM((tile_count, 2, depth, 4, 128), jnp.bfloat16),
             pltpu.SemaphoreType.DMA((tile_count, 2)),
             pltpu.SemaphoreType.DMA((2, tile_count)),
             pltpu.SemaphoreType.DMA((tile_count,)),
             pltpu.SemaphoreType.DMA((tile_count,)),
             pltpu.SemaphoreType.DMA((2,)),
+            pltpu.SemaphoreType.DMA((2, CHUNKS)),
+            pltpu.SemaphoreType.DMA((4, 2, CHUNKS)),
+            pltpu.SemaphoreType.DMA((4, 2, CHUNKS)),
         ],
         compiler_params=pltpu.CompilerParams(
-            collective_id=0, has_side_effects=True, vmem_limit_bytes=CAP_VMEM
+            collective_id=0, has_side_effects=True, vmem_limit_bytes=16 * 1024 * 1024
         ),
     )(starts, labels, sweep)
+    level = lax.axis_index("ground") // 4
+    where = jnp.stack([2 - level // 2, lax.axis_index("pair")]).astype(jnp.int32)
     looked = pl.pallas_call(
         functools.partial(combine_kernel, allowance),
-        grid=(tile_count,),
-        out_shape=jax.ShapeDtypeStruct((32, 128), jnp.float32),
-        in_specs=[
-            smem,
-            pl.BlockSpec((2, 1, allowance * half, 8, 128), lambda i: (0, i, 0, 0, 0)),
-            vmem, vmem, vmem,
-        ],
+        out_shape=jax.ShapeDtypeStruct((64, 128), jnp.float32),
+        in_specs=[smem, smem, vmem, vmem, vmem, vmem],
         out_specs=vmem,
         scratch_shapes=[
-            pltpu.VMEM((2, SLOTS, half, 8, 128), jnp.float32),
+            pltpu.VMEM((2, SLOTS, SHARD_HEIGHT, 4, 128), jnp.float32),
             pltpu.SMEM((SLOTS,), jnp.int32),
             pltpu.VMEM((2, 2, 256, 128), jnp.float32),
         ],
-        compiler_params=pltpu.CompilerParams(vmem_limit_bytes=CAP_VMEM),
-    )(arrived_labels, arrived, *pool)
+        compiler_params=pltpu.CompilerParams(vmem_limit_bytes=24 * 1024 * 1024),
+    )(where, arrived_labels, arrived, relayed, *pool)
     filtered = pl.pallas_call(
         filter_kernel,
         out_shape=jax.ShapeDtypeStruct((2, 64, 64), jnp.float32),
-        in_specs=[vmem] * 5,
+        in_specs=[vmem] * 4,
         out_specs=vmem,
         scratch_shapes=[
-            pltpu.VMEM((32, 128), jnp.float32),
+            pltpu.VMEM((64, 128), jnp.float32),
             pltpu.SemaphoreType.DMA,
             pltpu.SemaphoreType.DMA,
         ],
@@ -461,7 +557,7 @@
 
 
 def solution(mesh):
-    if mesh.shape["pair"] != 2:
+    if mesh.shape["pair"] != 2 or mesh.shape["ground"] != 16:
         return general(mesh)
     placed = (P("pair", "ground", None, None, None), P("ground"), P("ground", None), P("ground"))
     return jax.shard_map(

time: 124 us -> 121 us (0.976)
  the two profiles are of different devices: /device:TPU:16 before, /device:TPU:0 now
where the time goes in v2:
time: 121 us; the launch traced here: 120 us
  Pallas kernels  115 us (95%)
  local copies, waits for them, and re-layouts  4.57 us (4%)
    pallas_call x1, Pallas kernels, local_pair(): pl.pallas_call(functools.partial(exchange_kernel, allowance), out_shape=(...  95.5 us
    pallas_call x1, Pallas kernels, local_pair(): pl.pallas_call(filter_kernel, out_shape=jax.ShapeDtypeStruct((2, 64, 64),...  11.2 us
    pallas_call x1, Pallas kernels, local_pair(): pl.pallas_call(functools.partial(combine_kernel, allowance), out_shape=ja...  5.9 us
    pallas_call x1, Pallas kernels, local_pair(): pl.pallas_call(functools.partial(table_kernel, allowance), out_shape=(jax...  2.9 us
    another operation x2, local copies, waits for them, and re-layouts, local_pair(): sweep = coregistered_sweeps[0, 0].reshape(height, 2, 2, 2, 128).transpose...  2.47 us

profile of v2, /device:TPU:0, one launch (start us, length us, event | category | flops | bytes accessed | tf_op | source)
XLA Modules:
  0.0 120.2 jit_solution(8617586312859919185)
XLA Ops:
  0.0 0.0 copy-start.2
  0.0 0.0 copy-start
  0.0 0.1 pad_add_fusion.where
  0.1 2.9 %shard_map.91 = (s32[16,8]{1,0:T(8,128)}, s32[16,1,128]{2,1,0:T(1,128)}) custom-call(s32[64]{0:T(128)} %opening.1, s32[64]{0:T(128)} %bitcast.9, s32[64]{0:T(128)} %place.1), custom_call_target="tpu_custom_call" | custom-call | tf_op jit(solution)/shard_map/pallas_call | solution.py:489
  3.0 0.0 copy-start.3
  3.0 0.0 copy-start.4
  3.0 1.7 %reshape_squeeze.3 = bf16[512,2,2,2,128]{4,3,2,1,0:T(2,128)(2,1)S(1)} reshape(bf16[1,1,512,2,512]{4,3,2,1,0:T(2,128)(2,1)} %param.9) | data formatting | bytes 2097152 | tf_op jit(solution)/shard_map/reshape;squeeze | solution.py:501
  4.8 0.7 copy.10
  5.5 0.0 copy-done.3
  5.5 0.0 copy-done.4
  5.5 95.5 %shard_map.92 = (bf16[2,16,128,4,128]{4,3,2,1,0:T(4,128)(2,1)S(1)}, bf16[4,2,512,4,128]{4,3,2,1,0:T(4,128)(2,1)S(1)}, s32[16,1,128]{2,1,0:T(1,128)S(1)}) custom-call(s32[16,8]{1,0:T(8,128)S(1)} %copy-done.3, s32[16,1,128]{2,1,0:T(1,128)S(1)} %copy-done.4, bf16[2,512,4,128]{3,2,1,0:T(4,128)(2,1)S(1)} %bitcast.7), custom_call_target="tpu_custom_call" | custom-call | tf_op jit(solution)/shard_map/pallas_call | solution.py:506
  101.0 0.0 copy-done.2
  101.0 0.0 copy-done
  101.0 5.9 %shard_map.93.looked = f32[64,128]{1,0:T(8,128)S(1)} custom-call(s32[2]{0:T(128)S(1)} %pad_add_fusion.where, s32[16,1,128]{2,1,0:T(1,128)S(1)} %get-tuple-element.12.labels, bf16[2,16,128,4,128]{4,3,2,1,0:T(4,128)(2,1)S(1)} %get-tuple-element.13.arrived, bf16[4,2,512,4,128]{4,3,2,1,0:T(4,128)(2,1)S(1)} %get-tuple-element.14.relayed, ...), custom_call_target="tpu_custom_call" | custom-call | tf_op jit(solution)/shard_map/pallas_call | solution.py:532
  106.9 0.0 copy-start.1
  106.9 0.6 copy-done.1
  107.5 11.2 %shard_map.94 = f32[2,64,64]{2,1,0:T(8,128)} custom-call(f32[64,128]{1,0:T(8,128)} %copy-done.1, f32[128,64]{1,0:T(8,128)} %constant.45.clone.left, f32[128,128]{1,0:T(8,128)} %constant.46.clone.right, f32[128,128]{1,0:T(8,128)} %constant.47.clone.right_back), custom_call_target="tpu_custom_call" | custom-call | tf_op jit(solution)/shard_map/pallas_call | solution.py:544
  118.7 1.5 %copy.12 = f32[1,1,1,2,64,64]{5,4,3,2,1,0:T(8,128)} copy(f32[1,1,1,2,64,64]{5,4,3,2,1,0:T(8,128)} %bitcast.8) | data formatting | bytes 65536
Async XLA Ops:
  0.0 101.0 %copy-start.2 = (f32[64,256]{1,0:T(8,128)S(1)}, f32[64,256]{1,0:T(8,128)}, u32[]{:S(2)}) copy-start(f32[64,256]{1,0:T(8,128)} %constant.44.clone.gather) | copy-start | bytes 196612
  0.0 101.0 %copy-start = (f32[2,128,128]{2,1,0:T(8,128)S(1)}, f32[2,128,128]{2,1,0:T(8,128)}, u32[]{:S(2)}) copy-start(f32[2,128,128]{2,1,0:T(8,128)} %constant.43.clone.spread) | copy-start | bytes 393220
  3.0 2.5 %copy-start.3 = (s32[16,8]{1,0:T(8,128)S(1)}, s32[16,8]{1,0:T(8,128)}, u32[]{:S(2)}) copy-start(s32[16,8]{1,0:T(8,128)} %get-tuple-element.10.starts) | copy-start | bytes 1540
  3.0 2.5 %copy-start.4 = (s32[16,1,128]{2,1,0:T(1,128)S(1)}, s32[16,1,128]{2,1,0:T(1,128)}, u32[]{:S(2)}) copy-start(s32[16,1,128]{2,1,0:T(1,128)} %get-tuple-element.11.labels) | copy-start | bytes 24580
  106.9 0.6 copy-start.1

commit v3 on v2

--- a/solution.py
+++ b/solution.py
@@ -156,7 +156,7 @@
     )
 
 
-CHUNKS = 2
+CHUNKS = 4
 MESH = pl.DeviceIdType.MESH
 EXACT = lax.Precision.HIGHEST
 
@@ -293,14 +293,26 @@
             for part in range(2):
                 burst(part, chunk).start()
 
-    send(target_of(tile_count // 2))
-
-    def pairs(step, carry):
-        send(target_of(tile_count // 2 + step))
-        send(target_of(tile_count // 2 - step))
-        return carry
-
-    lax.fori_loop(1, tile_count // 2, pairs, 0)
+    mirror = level + right * (3 - 2 * level)
+
+    def near(step, carry):
+        distance = 1 - lax.rem(step, 2)
+        place = distance + mirror - 2 * distance * mirror
+        tile = (place + right * (3 - 2 * place)) * 4 + lax.rem(line + 1 + step // 2, 4)
+
+        @pl.when(tile != me)
+        def _():
+            send(tile)
+
+        return carry
+
+    def away(step, carry):
+        place = 3 - lax.rem(step, 2)
+        send((place + right * (3 - 2 * place)) * 4 + lax.rem(line + 1 + step // 2, 4))
+        return carry
+
+    lax.fori_loop(0, 8, near, 0)
+    lax.fori_loop(0, 8, away, 0)
     extract(me)
     parcel(me, 1 - mine, me, mine).start()
     own = pltpu.make_async_copy(outgoing.at[me, mine], arrived.at[mine, me], own_sem.at[0])

time: 121 us -> 116 us (0.959)
  the two profiles are of different devices: /device:TPU:0 before, /device:TPU:3 now
where the time goes in v3:
time: 116 us; the launch traced here: 114 us
  Pallas kernels  109 us (94%)
  local copies, waits for them, and re-layouts  4.57 us (4%)
    pallas_call x1, Pallas kernels, local_pair(): pl.pallas_call(functools.partial(exchange_kernel, allowance), out_shape=(...  90.8 us
    pallas_call x1, Pallas kernels, local_pair(): pl.pallas_call(filter_kernel, out_shape=jax.ShapeDtypeStruct((2, 64, 64),...  10.6 us
    pallas_call x1, Pallas kernels, local_pair(): pl.pallas_call(functools.partial(combine_kernel, allowance), out_shape=ja...  5.13 us
    pallas_call x1, Pallas kernels, local_pair(): pl.pallas_call(functools.partial(table_kernel, allowance), out_shape=(jax...  2.9 us
    another operation x2, local copies, waits for them, and re-layouts, local_pair(): sweep = coregistered_sweeps[0, 0].reshape(height, 2, 2, 2, 128).transpose...  2.47 us

profile of v3, /device:TPU:3, one launch (start us, length us, event | category | flops | bytes accessed | tf_op | source)
XLA Modules:
  0.0 114.2 jit_solution(5698191561114669215)
XLA Ops:
  0.0 0.0 copy-start.2
  0.0 0.0 copy-start
  0.0 0.1 pad_add_fusion.where
  0.1 2.9 %shard_map.91 = (s32[16,8]{1,0:T(8,128)}, s32[16,1,128]{2,1,0:T(1,128)}) custom-call(s32[64]{0:T(128)} %opening.1, s32[64]{0:T(128)} %bitcast.9, s32[64]{0:T(128)} %place.1), custom_call_target="tpu_custom_call" | custom-call | tf_op jit(solution)/shard_map/pallas_call | solution.py:501
  3.0 0.0 copy-start.3
  3.0 0.0 copy-start.4
  3.0 1.7 %reshape_squeeze.3 = bf16[512,2,2,2,128]{4,3,2,1,0:T(2,128)(2,1)S(1)} reshape(bf16[1,1,512,2,512]{4,3,2,1,0:T(2,128)(2,1)} %param.9) | data formatting | bytes 2097152 | tf_op jit(solution)/shard_map/reshape;squeeze | solution.py:513
  4.8 0.7 copy.10
  5.5 0.0 copy-done.3
  5.5 0.0 copy-done.4
  5.5 90.8 %shard_map.92 = (bf16[2,16,128,4,128]{4,3,2,1,0:T(4,128)(2,1)S(1)}, bf16[4,2,512,4,128]{4,3,2,1,0:T(4,128)(2,1)S(1)}, s32[16,1,128]{2,1,0:T(1,128)S(1)}) custom-call(s32[16,8]{1,0:T(8,128)S(1)} %copy-done.3, s32[16,1,128]{2,1,0:T(1,128)S(1)} %copy-done.4, bf16[2,512,4,128]{3,2,1,0:T(4,128)(2,1)S(1)} %bitcast.7), custom_call_target="tpu_custom_call" | custom-call | tf_op jit(solution)/shard_map/pallas_call | solution.py:518
  96.4 0.0 copy-done.2
  96.4 0.0 copy-done
  96.4 5.1 %shard_map.93.looked = f32[64,128]{1,0:T(8,128)S(1)} custom-call(s32[2]{0:T(128)S(1)} %pad_add_fusion.where, s32[16,1,128]{2,1,0:T(1,128)S(1)} %get-tuple-element.12.labels, bf16[2,16,128,4,128]{4,3,2,1,0:T(4,128)(2,1)S(1)} %get-tuple-element.13.arrived, bf16[4,2,512,4,128]{4,3,2,1,0:T(4,128)(2,1)S(1)} %get-tuple-element.14.relayed, ...), custom_call_target="tpu_custom_call" | custom-call | tf_op jit(solution)/shard_map/pallas_call | solution.py:544
  101.5 0.0 copy-start.1
  101.5 0.6 copy-done.1
  102.1 10.6 %shard_map.94 = f32[2,64,64]{2,1,0:T(8,128)} custom-call(f32[64,128]{1,0:T(8,128)} %copy-done.1, f32[128,64]{1,0:T(8,128)} %constant.45.clone.left, f32[128,128]{1,0:T(8,128)} %constant.46.clone.right, f32[128,128]{1,0:T(8,128)} %constant.47.clone.right_back), custom_call_target="tpu_custom_call" | custom-call | tf_op jit(solution)/shard_map/pallas_call | solution.py:556
  112.7 1.5 %copy.12 = f32[1,1,1,2,64,64]{5,4,3,2,1,0:T(8,128)} copy(f32[1,1,1,2,64,64]{5,4,3,2,1,0:T(8,128)} %bitcast.8) | data formatting | bytes 65536
Async XLA Ops:
  0.0 96.4 %copy-start.2 = (f32[64,256]{1,0:T(8,128)S(1)}, f32[64,256]{1,0:T(8,128)}, u32[]{:S(2)}) copy-start(f32[64,256]{1,0:T(8,128)} %constant.44.clone.gather) | copy-start | bytes 196612
  0.0 96.4 %copy-start = (f32[2,128,128]{2,1,0:T(8,128)S(1)}, f32[2,128,128]{2,1,0:T(8,128)}, u32[]{:S(2)}) copy-start(f32[2,128,128]{2,1,0:T(8,128)} %constant.43.clone.spread) | copy-start | bytes 393220
  3.0 2.5 %copy-start.3 = (s32[16,8]{1,0:T(8,128)S(1)}, s32[16,8]{1,0:T(8,128)}, u32[]{:S(2)}) copy-start(s32[16,8]{1,0:T(8,128)} %get-tuple-element.10.starts) | copy-start | bytes 1540
  3.0 2.5 %copy-start.4 = (s32[16,1,128]{2,1,0:T(1,128)S(1)}, s32[16,1,128]{2,1,0:T(1,128)}, u32[]{:S(2)}) copy-start(s32[16,1,128]{2,1,0:T(1,128)} %get-tuple-element.11.labels) | copy-start | bytes 24580
  101.5 0.6 copy-start.1

commit v4 on v3

--- a/solution.py
+++ b/solution.py
@@ -156,7 +156,6 @@
     )
 
 
-CHUNKS = 4
 MESH = pl.DeviceIdType.MESH
 EXACT = lax.Precision.HIGHEST
 
@@ -187,21 +186,17 @@
 
 
 def exchange_kernel(
-    allowance, starts, labels, sweep, arrived, relayed, arrived_labels,
+    allowance, starts, labels, sweep, arrived, arrived_labels,
     outgoing, send_sem, recv_sem, label_send, label_recv, own_sem,
-    burst_send, relay_send, relay_recv,
+    first_half, second_half, proxied, far_table, far_starts, burst_send, burst_recv, table_sem, proxy_sem,
 ):
     me = lax.axis_index("ground")
     mine = lax.axis_index("pair")
     tile_count = 16
     level = me // 4
     line = lax.rem(me, 4)
-    across = lax.rem(line + 2, 4)
-    beside = line + 1 - 2 * lax.rem(line, 2)
-    across_beside = lax.rem(beside + 2, 4)
     inner = jnp.logical_or(level == 1, level == 2)
     right = level // 2
-    outward = 3 * right
     far = 2 - right
     barrier = pltpu.get_barrier_semaphore()
 
@@ -246,28 +241,44 @@
             device_id_type=MESH,
         )
 
-    span = sweep.shape[1] // CHUNKS
-
-    def burst(part, chunk):
-        rows = pl.ds(chunk * span, span)
+    far_me = far * 4 + line
+
+    halves = (first_half, second_half)
+
+    def burst(part, pair):
         return pltpu.make_async_remote_copy(
-            src_ref=sweep.at[part, rows],
-            dst_ref=relayed.at[line, mine, rows],
-            send_sem=burst_send.at[part, chunk],
-            recv_sem=relay_recv.at[line, mine, chunk],
-            device_id={"ground": far * 4 + line, "pair": part},
+            src_ref=sweep.at[part],
+            dst_ref=halves[pair],
+            send_sem=burst_send.at[part],
+            recv_sem=burst_recv.at[pair],
+            device_id={"ground": far_me, "pair": part},
             device_id_type=MESH,
         )
 
-    def relay(kind, which, target, pair, chunk):
-        rows = pl.ds(chunk * span, span)
+    def far_rows():
         return pltpu.make_async_remote_copy(
-            src_ref=relayed.at[which, pair, rows],
-            dst_ref=relayed.at[which, pair, rows],
-            send_sem=relay_send.at[kind, pair, chunk],
-            recv_sem=relay_recv.at[which, pair, chunk],
-            device_id={"ground": target, "pair": mine},
+            src_ref=labels.at[pl.ds(8 * (1 - right), 8)],
+            dst_ref=far_table,
+            send_sem=table_sem.at[0],
+            recv_sem=table_sem.at[1],
+            device_id={"ground": far_me, "pair": mine},
             device_id_type=MESH,
+        )
+
+    def proxy(index, pair):
+        return pltpu.make_async_remote_copy(
+            src_ref=proxied.at[index, pair],
+            dst_ref=arrived.at[pair, far_me],
+            send_sem=proxy_sem.at[index, pair],
+            recv_sem=recv_sem.at[pair, far_me],
+            device_id={"ground": 8 * right + index, "pair": mine},
+            device_id_type=MESH,
+        )
+
+    def proxy_own(pair):
+        index = me - 8 * right
+        return pltpu.make_async_copy(
+            proxied.at[index, pair], arrived.at[pair, far_me], proxy_sem.at[index, pair]
         )
 
     def target_of(step):
@@ -289,9 +300,13 @@
 
     @pl.when(inner)
     def _():
-        for chunk in range(CHUNKS):
-            for part in range(2):
-                burst(part, chunk).start()
+        far_rows().start()
+        for pair in range(2):
+
+            @pl.when(mine == pair)
+            def _():
+                for part in range(2):
+                    burst(part, pair).start()
 
     mirror = level + right * (3 - 2 * level)
 
@@ -320,45 +335,46 @@
     own_tag = pltpu.make_async_copy(labels.at[me], arrived_labels.at[me], own_sem.at[1])
     own_tag.start()
 
-    base = level * 4
-    order = [(pair, chunk) for chunk in range(CHUNKS) for pair in range(2)]
-
-    def second(pair, chunk):
-        relay(1, across, base + across, pair, chunk).wait_recv()
-        relay(3, across, base + beside, pair, chunk).start()
-
-    for spot, (pair, chunk) in enumerate(order):
-        relay(0, line, base + across, pair, chunk).wait_recv()
-
-        @pl.when(inner)
-        def _():
-            relay(0, line, outward * 4 + line, pair, chunk).start()
-
-        relay(1, line, base + across, pair, chunk).start()
-        relay(2, line, base + beside, pair, chunk).start()
-        if spot:
-            second(*order[spot - 1])
-    second(*order[-1])
-
-    for pair, chunk in order:
-        relay(2, beside, base + beside, pair, chunk).wait_recv()
-        relay(3, across_beside, base + beside, pair, chunk).wait_recv()
-
-        @pl.when(inner)
-        def _():
-            relay(0, line, outward * 4 + line, pair, chunk).wait_send()
-            burst(pair, chunk).wait_send()
-
-        relay(1, line, base + across, pair, chunk).wait_send()
-        relay(2, line, base + beside, pair, chunk).wait_send()
-        relay(3, across, base + beside, pair, chunk).wait_send()
+    @pl.when(inner)
+    def _():
+        far_rows().wait()
+        rows = pltpu.make_async_copy(far_table, far_starts, table_sem.at[2])
+        rows.start()
+        rows.wait()
+
+        for pair in range(2):
+            burst(0, pair).wait_recv()
+
+            def one_tile(step, carry):
+                index = lax.rem(4 * right + step, 8)
+
+                def one(slot, carry):
+                    top = far_starts[index, 0, 2 * allowance + slot]
+                    proxied[index, pair, pl.ds(slot * SHARD_HEIGHT, SHARD_HEIGHT)] = halves[pair][
+                        pl.ds(top, SHARD_HEIGHT)
+                    ]
+                    return carry
+
+                lax.fori_loop(0, allowance, one, 0)
+
+                @pl.when(8 * right + index != me)
+                def _():
+                    proxy(index, pair).start()
+
+                @pl.when(8 * right + index == me)
+                def _():
+                    proxy_own(pair).start()
+
+                return carry
+
+            lax.fori_loop(0, 8, one_tile, 0)
 
     def finish(step, carry):
         tile = target_of(step)
         tag(tile, tile).wait_recv()
         tag(tile, me).wait_send()
 
-        @pl.when(tile // 4 != far)
+        @pl.when(jnp.logical_or(jnp.logical_not(inner), tile != far_me))
         def _():
             parcel(tile, 1 - mine, tile, 1 - mine).wait_recv()
             parcel(tile, mine, tile, mine).wait_recv()
@@ -376,15 +392,33 @@
     own.wait()
     own_tag.wait()
 
-
-def combine_kernel(allowance, where, labels, arrived, relayed, spread, gather, looked, total, count, prods):
-    far = where[0]
-    mine = where[1]
+    @pl.when(inner)
+    def _():
+        def settle(index, carry):
+            for pair in range(2):
+
+                @pl.when(8 * right + index != me)
+                def _():
+                    proxy(index, pair).wait_send()
+
+                @pl.when(8 * right + index == me)
+                def _():
+                    proxy_own(pair).wait()
+
+            return carry
+
+        lax.fori_loop(0, 8, settle, 0)
+        for part in range(2):
+            burst(part, 0).wait_send()
+
+
+def combine_kernel(allowance, where, labels, arrived, spread, gather, looked, total, count, prods):
+    mine = where[0]
     total[...] = jnp.zeros_like(total)
     for slot in range(SLOTS):
         count[slot] = 0
 
-    def add(source, load):
+    def one_source(source, carry):
         for slot in range(allowance):
             label = labels[source, 0, slot]
 
@@ -392,20 +426,8 @@
             def _():
                 count[label - 1] = count[label - 1] + 1
                 for part in range(2):
-                    total[part, label - 1] += load(part, slot).astype(jnp.float32)
-
-    def one_source(source, carry):
-        @pl.when(source // 4 != far)
-        def _():
-            add(source, lambda part, slot: arrived[part, source, pl.ds(slot * SHARD_HEIGHT, SHARD_HEIGHT)])
-
-        @pl.when(source // 4 == far)
-        def _():
-            def load(part, slot):
-                top = labels[source, 0, 2 * allowance + slot]
-                return relayed[lax.rem(source, 4), part, pl.ds(top, SHARD_HEIGHT)]
-
-            add(source, load)
+                    piece = arrived[part, source, pl.ds(slot * SHARD_HEIGHT, SHARD_HEIGHT)]
+                    total[part, label - 1] += piece.astype(jnp.float32)
 
         return carry
 
@@ -515,15 +537,14 @@
         .reshape(2, height, 4, 128)
     )
     depth = allowance * SHARD_HEIGHT
-    arrived, relayed, arrived_labels = pl.pallas_call(
+    arrived, arrived_labels = pl.pallas_call(
         functools.partial(exchange_kernel, allowance),
         out_shape=(
             jax.ShapeDtypeStruct((2, tile_count, depth, 4, 128), jnp.bfloat16),
-            jax.ShapeDtypeStruct((4, 2, height, 4, 128), jnp.bfloat16),
             jax.ShapeDtypeStruct((tile_count, 1, 128), jnp.int32),
         ),
         in_specs=[smem, vmem, vmem],
-        out_specs=(anyplace, anyplace, vmem),
+        out_specs=(anyplace, vmem),
         scratch_shapes=[
             pltpu.VMEM((tile_count, 2, depth, 4, 128), jnp.bfloat16),
             pltpu.SemaphoreType.DMA((tile_count, 2)),
@@ -531,20 +552,25 @@
             pltpu.SemaphoreType.DMA((tile_count,)),
             pltpu.SemaphoreType.DMA((tile_count,)),
             pltpu.SemaphoreType.DMA((2,)),
-            pltpu.SemaphoreType.DMA((2, CHUNKS)),
-            pltpu.SemaphoreType.DMA((4, 2, CHUNKS)),
-            pltpu.SemaphoreType.DMA((4, 2, CHUNKS)),
+            pltpu.VMEM((height, 4, 128), jnp.bfloat16),
+            pltpu.VMEM((height, 4, 128), jnp.bfloat16),
+            pltpu.VMEM((8, 2, depth, 4, 128), jnp.bfloat16),
+            pltpu.VMEM((8, 1, 128), jnp.int32),
+            pltpu.SMEM((8, 1, 128), jnp.int32),
+            pltpu.SemaphoreType.DMA((2,)),
+            pltpu.SemaphoreType.DMA((2,)),
+            pltpu.SemaphoreType.DMA((3,)),
+            pltpu.SemaphoreType.DMA((8, 2)),
         ],
         compiler_params=pltpu.CompilerParams(
             collective_id=0, has_side_effects=True, vmem_limit_bytes=16 * 1024 * 1024
         ),
     )(starts, labels, sweep)
-    level = lax.axis_index("ground") // 4
-    where = jnp.stack([2 - level // 2, lax.axis_index("pair")]).astype(jnp.int32)
+    where = lax.axis_index("pair").astype(jnp.int32)[None]
     looked = pl.pallas_call(
         functools.partial(combine_kernel, allowance),
         out_shape=jax.ShapeDtypeStruct((64, 128), jnp.float32),
-        in_specs=[smem, smem, vmem, vmem, vmem, vmem],
+        in_specs=[smem, smem, vmem, vmem, vmem],
         out_specs=vmem,
         scratch_shapes=[
             pltpu.VMEM((2, SLOTS, SHARD_HEIGHT, 4, 128), jnp.float32),
@@ -552,7 +578,7 @@
             pltpu.VMEM((2, 2, 256, 128), jnp.float32),
         ],
         compiler_params=pltpu.CompilerParams(vmem_limit_bytes=24 * 1024 * 1024),
-    )(where, arrived_labels, arrived, relayed, *pool)
+    )(where, arrived_labels, arrived, *pool)
     filtered = pl.pallas_call(
         filter_kernel,
         out_shape=jax.ShapeDtypeStruct((2, 64, 64), jnp.float32),

time: 116 us -> 131 us (1.13)
  Pallas kernels: 109 us -> 122 us
  local copies, waits for them, and re-layouts: 4.57 us -> 8.69 us
    pallas_call x1, Pallas kernels: 10.6 us -> 28.9 us  [local_pair(): pl.pallas_call(filter_kernel, out_shape=jax.ShapeDtypeStruct((2, 64, 64),...]
    pallas_call x1, Pallas kernels: 90.8 us -> 85 us  [local_pair(): pl.pallas_call(functools.partial(exchange_kernel, allowance), out_shape=(...]
    unnamed x11 -> x15, local copies, waits for them, and re-layouts: 2.1 us -> 6.22 us
where the time goes in v4:
time: 131 us; the launch traced here: 130 us
  Pallas kernels  122 us (93%)
  local copies, waits for them, and re-layouts  8.69 us (7%)
    pallas_call x1, Pallas kernels, local_pair(): pl.pallas_call(functools.partial(exchange_kernel, allowance), out_shape=(...  85 us
    pallas_call x1, Pallas kernels, local_pair(): pl.pallas_call(filter_kernel, out_shape=jax.ShapeDtypeStruct((2, 64, 64),...  28.9 us
    unnamed x15, local copies, waits for them, and re-layouts  6.22 us
    pallas_call x1, Pallas kernels, local_pair(): pl.pallas_call(functools.partial(combine_kernel, allowance), out_shape=ja...  4.78 us
    pallas_call x1, Pallas kernels, local_pair(): pl.pallas_call(functools.partial(table_kernel, allowance), out_shape=(jax...  2.9 us

profile of v4, /device:TPU:3, one launch (start us, length us, event | category | flops | bytes accessed | tf_op | source)
XLA Modules:
  0.0 130.3 jit_solution(5278856444677474752)
XLA Ops:
  0.0 0.0 copy-start.3
  0.0 0.0 copy-start.4
  0.0 2.9 %shard_map.91 = (s32[16,8]{1,0:T(8,128)}, s32[16,1,128]{2,1,0:T(1,128)}) custom-call(s32[64]{0:T(128)} %opening.1, s32[64]{0:T(128)} %bitcast.8, s32[64]{0:T(128)} %place.1), custom_call_target="tpu_custom_call" | custom-call | tf_op jit(solution)/shard_map/pallas_call | solution.py:523
  2.9 0.0 copy-start.5
  2.9 0.0 copy-start.6
  2.9 1.7 %reshape_squeeze.3 = bf16[512,2,2,2,128]{4,3,2,1,0:T(2,128)(2,1)S(1)} reshape(bf16[1,1,512,2,512]{4,3,2,1,0:T(2,128)(2,1)} %param.9) | data formatting | bytes 2097152 | tf_op jit(solution)/shard_map/reshape;squeeze | solution.py:535
  4.7 0.7 copy.10
  5.4 0.0 copy-done.5
  5.4 0.0 copy-done.6
  5.4 85.0 %shard_map.92 = (bf16[2,16,128,4,128]{4,3,2,1,0:T(4,128)(2,1)S(1)}, s32[16,1,128]{2,1,0:T(1,128)S(1)}) custom-call(s32[16,8]{1,0:T(8,128)S(1)} %copy-done.5, s32[16,1,128]{2,1,0:T(1,128)S(1)} %copy-done.6, bf16[2,512,4,128]{3,2,1,0:T(4,128)(2,1)S(1)} %bitcast.6), custom_call_target="tpu_custom_call" | custom-call | tf_op jit(solution)/shard_map/pallas_call | solution.py:540
  90.4 0.0 copy-start
  90.4 1.9 %copy-done = bf16[2,16,128,4,128]{4,3,2,1,0:T(4,128)(2,1)} copy-done((bf16[2,16,128,4,128]{4,3,2,1,0:T(4,128)(2,1)}, bf16[2,16,128,4,128]{4,3,2,1,0:T(4,128)(2,1)S(1)}, u32[]{:S(2)}) %copy-start) | copy-done | bytes 4194328
  92.3 0.0 copy-done.3
  92.3 0.0 copy-done.4
  92.3 0.0 copy-start.1
  92.4 2.2 %copy-done.1 = bf16[2,16,128,4,128]{4,3,2,1,0:T(4,128)(2,1)S(1)} copy-done((bf16[2,16,128,4,128]{4,3,2,1,0:T(4,128)(2,1)S(1)}, bf16[2,16,128,4,128]{4,3,2,1,0:T(4,128)(2,1)}, u32[]{:S(2)}) %copy-start.1) | copy-done | bytes 4194328
  94.5 4.8 %shard_map.93.looked = f32[64,128]{1,0:T(8,128)S(1)} custom-call(s32[1]{0:T(128)} %bitcast.where, s32[16,1,128]{2,1,0:T(1,128)S(1)} %get-tuple-element.11.labels, bf16[2,16,128,4,128]{4,3,2,1,0:T(4,128)(2,1)S(1)} %copy-done.1, f32[2,128,128]{2,1,0:T(8,128)S(1)} %copy-done.3, f32[64,256]{1,0:T(8,128)S(1)} %copy-done.4), custom_call_target="tpu_custom_call" | custom-call | tf_op jit(solution)/shard_map/pallas_call | solution.py:570
  99.3 0.0 copy-start.2
  99.3 0.6 copy-done.2
  99.9 28.9 %shard_map.94 = f32[2,64,64]{2,1,0:T(8,128)} custom-call(f32[64,128]{1,0:T(8,128)} %copy-done.2, f32[128,64]{1,0:T(8,128)} %constant.16.clone.left, f32[128,128]{1,0:T(8,128)} %constant.17.clone.right, f32[128,128]{1,0:T(8,128)} %constant.18.clone.right_back), custom_call_target="tpu_custom_call" | custom-call | tf_op jit(solution)/shard_map/pallas_call | solution.py:582
  128.8 1.5 %copy.12 = f32[1,1,1,2,64,64]{5,4,3,2,1,0:T(8,128)} copy(f32[1,1,1,2,64,64]{5,4,3,2,1,0:T(8,128)} %bitcast.7) | data formatting | bytes 65536
Async XLA Ops:
  0.0 92.3 %copy-start.3 = (f32[2,128,128]{2,1,0:T(8,128)S(1)}, f32[2,128,128]{2,1,0:T(8,128)}, u32[]{:S(2)}) copy-start(f32[2,128,128]{2,1,0:T(8,128)} %constant.14.clone.spread) | copy-start | bytes 393220
  0.0 92.3 %copy-start.4 = (f32[64,256]{1,0:T(8,128)S(1)}, f32[64,256]{1,0:T(8,128)}, u32[]{:S(2)}) copy-start(f32[64,256]{1,0:T(8,128)} %constant.15.clone.gather) | copy-start | bytes 196612
  2.9 2.5 %copy-start.5 = (s32[16,8]{1,0:T(8,128)S(1)}, s32[16,8]{1,0:T(8,128)}, u32[]{:S(2)}) copy-start(s32[16,8]{1,0:T(8,128)} %get-tuple-element.9.starts) | copy-start | bytes 1540
  2.9 2.5 %copy-start.6 = (s32[16,1,128]{2,1,0:T(1,128)S(1)}, s32[16,1,128]{2,1,0:T(1,128)}, u32[]{:S(2)}) copy-start(s32[16,1,128]{2,1,0:T(1,128)} %get-tuple-element.10.labels) | copy-start | bytes 24580
  90.4 1.9 %copy-start = (bf16[2,16,128,4,128]{4,3,2,1,0:T(4,128)(2,1)}, bf16[2,16,128,4,128]{4,3,2,1,0:T(4,128)(2,1)S(1)}, u32[]{:S(2)}) copy-start(bf16[2,16,128,4,128]{4,3,2,1,0:T(4,128)(2,1)S(1)} %get-tuple-element.12.arrived) | copy-start | bytes 12582916
  92.3 2.2 %copy-start.1 = (bf16[2,16,128,4,128]{4,3,2,1,0:T(4,128)(2,1)S(1)}, bf16[2,16,128,4,128]{4,3,2,1,0:T(4,128)(2,1)}, u32[]{:S(2)}) copy-start(bf16[2,16,128,4,128]{4,3,2,1,0:T(4,128)(2,1)} %copy-done) | copy-start | bytes 12582916
  99.3 0.6 copy-start.2

commit v5 on v4

--- a/solution.py
+++ b/solution.py
@@ -305,7 +305,7 @@
 
             @pl.when(mine == pair)
             def _():
-                for part in range(2):
+                for part in (pair, 1 - pair):
                     burst(part, pair).start()
 
     mirror = level + right * (3 - 2 * level)
@@ -342,7 +342,7 @@
         rows.start()
         rows.wait()
 
-        for pair in range(2):
+        def serve(pair):
             burst(0, pair).wait_recv()
 
             def one_tile(step, carry):
@@ -369,6 +369,13 @@
 
             lax.fori_loop(0, 8, one_tile, 0)
 
+        for first in range(2):
+
+            @pl.when(mine == first)
+            def _():
+                serve(first)
+                serve(1 - first)
+
     def finish(step, carry):
         tile = target_of(step)
         tag(tile, tile).wait_recv()
@@ -412,8 +419,8 @@
             burst(part, 0).wait_send()
 
 
-def combine_kernel(allowance, where, labels, arrived, spread, gather, looked, total, count, prods):
-    mine = where[0]
+def combine_kernel(allowance, labels, arrived, spread, gather, looked, total, count, prods):
+    mine = lax.axis_index("pair")
     total[...] = jnp.zeros_like(total)
     for slot in range(SLOTS):
         count[slot] = 0
@@ -563,22 +570,21 @@
             pltpu.SemaphoreType.DMA((8, 2)),
         ],
         compiler_params=pltpu.CompilerParams(
-            collective_id=0, has_side_effects=True, vmem_limit_bytes=16 * 1024 * 1024
+            collective_id=0, has_side_effects=True, vmem_limit_bytes=9 * 1024 * 1024
         ),
     )(starts, labels, sweep)
-    where = lax.axis_index("pair").astype(jnp.int32)[None]
     looked = pl.pallas_call(
         functools.partial(combine_kernel, allowance),
         out_shape=jax.ShapeDtypeStruct((64, 128), jnp.float32),
-        in_specs=[smem, smem, vmem, vmem, vmem],
+        in_specs=[smem, vmem, vmem, vmem],
         out_specs=vmem,
         scratch_shapes=[
             pltpu.VMEM((2, SLOTS, SHARD_HEIGHT, 4, 128), jnp.float32),
             pltpu.SMEM((SLOTS,), jnp.int32),
             pltpu.VMEM((2, 2, 256, 128), jnp.float32),
         ],
-        compiler_params=pltpu.CompilerParams(vmem_limit_bytes=24 * 1024 * 1024),
-    )(where, arrived_labels, arrived, *pool)
+        compiler_params=pltpu.CompilerParams(vmem_limit_bytes=12 * 1024 * 1024),
+    )(arrived_labels, arrived, *pool)
     filtered = pl.pallas_call(
         filter_kernel,
         out_shape=jax.ShapeDtypeStruct((2, 64, 64), jnp.float32),

time: 131 us -> 116 us (0.89)
  Pallas kernels: 122 us -> 111 us
  local copies, waits for them, and re-layouts: 8.69 us -> 4.57 us
    pallas_call x1, Pallas kernels: 28.9 us -> 5.62 us  [local_pair(): pl.pallas_call(filter_kernel, out_shape=jax.ShapeDtypeStruct((2, 64, 64),...]
    pallas_call x1, Pallas kernels: 85 us -> 97.2 us  [local_pair(): pl.pallas_call(functools.partial(exchange_kernel, allowance), out_shape=(...]
    unnamed x15 -> x11, local copies, waits for them, and re-layouts: 6.22 us -> 2.1 us
where the time goes in v5:
time: 116 us
  Pallas kernels  111 us (96%)
  local copies, waits for them, and re-layouts  4.57 us (4%)
    pallas_call x1, Pallas kernels, local_pair(): pl.pallas_call(functools.partial(exchange_kernel, allowance), out_shape=(...  97.2 us
    pallas_call x1, Pallas kernels, local_pair(): pl.pallas_call(filter_kernel, out_shape=jax.ShapeDtypeStruct((2, 64, 64),...  5.62 us
    pallas_call x1, Pallas kernels, local_pair(): pl.pallas_call(functools.partial(combine_kernel, allowance), out_shape=ja...  5.29 us
    pallas_call x1, Pallas kernels, local_pair(): pl.pallas_call(functools.partial(table_kernel, allowance), out_shape=(jax...  2.9 us
    another operation x2, local copies, waits for them, and re-layouts, local_pair(): sweep = coregistered_sweeps[0, 0].reshape(height, 2, 2, 2, 128).transpose...  2.47 us

profile of v5, /device:TPU:3, one launch (start us, length us, event | category | flops | bytes accessed | tf_op | source)
XLA Modules:
  0.0 115.7 jit_solution(10961462762529474678)
XLA Ops:
  0.0 0.0 copy-start.2
  0.0 0.0 copy-start.1
  0.0 2.9 %shard_map.91 = (s32[16,8]{1,0:T(8,128)}, s32[16,1,128]{2,1,0:T(1,128)}) custom-call(s32[64]{0:T(128)} %opening.1, s32[64]{0:T(128)} %bitcast.7, s32[64]{0:T(128)} %place.1), custom_call_target="tpu_custom_call" | custom-call | tf_op jit(solution)/shard_map/pallas_call | solution.py:530
  2.9 0.0 copy-start.3
  2.9 0.0 copy-start.4
  2.9 1.7 %reshape_squeeze.3 = bf16[512,2,2,2,128]{4,3,2,1,0:T(2,128)(2,1)S(1)} reshape(bf16[1,1,512,2,512]{4,3,2,1,0:T(2,128)(2,1)} %param.9) | data formatting | bytes 2097152 | tf_op jit(solution)/shard_map/reshape;squeeze | solution.py:542
  4.7 0.7 copy.10
  5.4 0.0 copy-done.3
  5.4 0.0 copy-done.4
  5.4 97.2 %shard_map.92 = (bf16[2,16,128,4,128]{4,3,2,1,0:T(4,128)(2,1)S(1)}, s32[16,1,128]{2,1,0:T(1,128)S(1)}) custom-call(s32[16,8]{1,0:T(8,128)S(1)} %copy-done.3, s32[16,1,128]{2,1,0:T(1,128)S(1)} %copy-done.4, bf16[2,512,4,128]{3,2,1,0:T(4,128)(2,1)S(1)} %bitcast.5), custom_call_target="tpu_custom_call" | custom-call | tf_op jit(solution)/shard_map/pallas_call | solution.py:547
  102.7 0.0 copy-done.2
  102.7 0.0 copy-done.1
  102.7 5.3 %shard_map.93.looked = f32[64,128]{1,0:T(8,128)S(1)} custom-call(s32[16,1,128]{2,1,0:T(1,128)S(1)} %get-tuple-element.11.labels, bf16[2,16,128,4,128]{4,3,2,1,0:T(4,128)(2,1)S(1)} %get-tuple-element.12.arrived, f32[2,128,128]{2,1,0:T(8,128)S(1)} %copy-done.1, f32[64,256]{1,0:T(8,128)S(1)} %copy-done.2), custom_call_target="tpu_custom_call" | custom-call | tf_op jit(solution)/shard_map/pallas_call | solution.py:576
  108.0 0.0 copy-start
  108.0 0.6 copy-done
  108.6 5.6 %shard_map.94 = f32[2,64,64]{2,1,0:T(8,128)} custom-call(f32[64,128]{1,0:T(8,128)} %copy-done, f32[128,64]{1,0:T(8,128)} %constant.12.clone.left, f32[128,128]{1,0:T(8,128)} %constant.13.clone.right, f32[128,128]{1,0:T(8,128)} %constant.14.clone.right_back), custom_call_target="tpu_custom_call" | custom-call | tf_op jit(solution)/shard_map/pallas_call | solution.py:588
  114.2 1.5 %copy.12 = f32[1,1,1,2,64,64]{5,4,3,2,1,0:T(8,128)} copy(f32[1,1,1,2,64,64]{5,4,3,2,1,0:T(8,128)} %bitcast.6) | data formatting | bytes 65536
Async XLA Ops:
  0.0 102.7 %copy-start.2 = (f32[64,256]{1,0:T(8,128)S(1)}, f32[64,256]{1,0:T(8,128)}, u32[]{:S(2)}) copy-start(f32[64,256]{1,0:T(8,128)} %constant.11.clone.gather) | copy-start | bytes 196612
  0.0 102.7 %copy-start.1 = (f32[2,128,128]{2,1,0:T(8,128)S(1)}, f32[2,128,128]{2,1,0:T(8,128)}, u32[]{:S(2)}) copy-start(f32[2,128,128]{2,1,0:T(8,128)} %constant.10.clone.spread) | copy-start | bytes 393220
  2.9 2.5 %copy-start.3 = (s32[16,8]{1,0:T(8,128)S(1)}, s32[16,8]{1,0:T(8,128)}, u32[]{:S(2)}) copy-start(s32[16,8]{1,0:T(8,128)} %get-tuple-element.9.starts) | copy-start | bytes 1540
  2.9 2.5 %copy-start.4 = (s32[16,1,128]{2,1,0:T(1,128)S(1)}, s32[16,1,128]{2,1,0:T(1,128)}, u32[]{:S(2)}) copy-start(s32[16,1,128]{2,1,0:T(1,128)} %get-tuple-element.10.labels) | copy-start | bytes 24580
  108.0 0.6 copy-start

commit v6 on v5

--- a/solution.py
+++ b/solution.py
@@ -156,6 +156,7 @@
     )
 
 
+CHUNKS = 8
 MESH = pl.DeviceIdType.MESH
 EXACT = lax.Precision.HIGHEST
 
@@ -245,12 +246,15 @@
 
     halves = (first_half, second_half)
 
-    def burst(part, pair):
+    span = sweep.shape[1] // CHUNKS
+
+    def burst(part, pair, chunk):
+        rows = pl.ds(chunk * span, span)
         return pltpu.make_async_remote_copy(
-            src_ref=sweep.at[part],
-            dst_ref=halves[pair],
-            send_sem=burst_send.at[part],
-            recv_sem=burst_recv.at[pair],
+            src_ref=sweep.at[part, rows],
+            dst_ref=halves[pair].at[rows],
+            send_sem=burst_send.at[part, chunk],
+            recv_sem=burst_recv.at[pair, chunk],
             device_id={"ground": far_me, "pair": part},
             device_id_type=MESH,
         )
@@ -306,7 +310,8 @@
             @pl.when(mine == pair)
             def _():
                 for part in (pair, 1 - pair):
-                    burst(part, pair).start()
+                    for chunk in range(CHUNKS):
+                        burst(part, pair, chunk).start()
 
     mirror = level + right * (3 - 2 * level)
 
@@ -343,7 +348,8 @@
         rows.wait()
 
         def serve(pair):
-            burst(0, pair).wait_recv()
+            for chunk in range(CHUNKS):
+                burst(0, pair, chunk).wait_recv()
 
             def one_tile(step, carry):
                 index = lax.rem(4 * right + step, 8)
@@ -416,7 +422,8 @@
 
         lax.fori_loop(0, 8, settle, 0)
         for part in range(2):
-            burst(part, 0).wait_send()
+            for chunk in range(CHUNKS):
+                burst(part, 0, chunk).wait_send()
 
 
 def combine_kernel(allowance, labels, arrived, spread, gather, looked, total, count, prods):
@@ -564,8 +571,8 @@
             pltpu.VMEM((8, 2, depth, 4, 128), jnp.bfloat16),
             pltpu.VMEM((8, 1, 128), jnp.int32),
             pltpu.SMEM((8, 1, 128), jnp.int32),
-            pltpu.SemaphoreType.DMA((2,)),
-            pltpu.SemaphoreType.DMA((2,)),
+            pltpu.SemaphoreType.DMA((2, CHUNKS)),
+            pltpu.SemaphoreType.DMA((2, CHUNKS)),
             pltpu.SemaphoreType.DMA((3,)),
             pltpu.SemaphoreType.DMA((8, 2)),
         ],

time: 116 us -> 116 us (level)
  no operation moved by 1% of the time
where the time goes in v6:
time: 116 us
  Pallas kernels  111 us (96%)
  local copies, waits for them, and re-layouts  4.57 us (4%)
    pallas_call x1, Pallas kernels, local_pair(): pl.pallas_call(functools.partial(exchange_kernel, allowance), out_shape=(...  97.5 us
    pallas_call x1, Pallas kernels, local_pair(): pl.pallas_call(filter_kernel, out_shape=jax.ShapeDtypeStruct((2, 64, 64),...  5.62 us
    pallas_call x1, Pallas kernels, local_pair(): pl.pallas_call(functools.partial(combine_kernel, allowance), out_shape=ja...  5.39 us
    pallas_call x1, Pallas kernels, local_pair(): pl.pallas_call(functools.partial(table_kernel, allowance), out_shape=(jax...  2.9 us
    another operation x2, local copies, waits for them, and re-layouts, local_pair(): sweep = coregistered_sweeps[0, 0].reshape(height, 2, 2, 2, 128).transpose...  2.47 us

profile of v6, /device:TPU:3, one launch (start us, length us, event | category | flops | bytes accessed | tf_op | source)
XLA Modules:
  0.0 116.0 jit_solution(1154124401821797694)
XLA Ops:
  0.0 0.0 copy-start.2
  0.0 0.0 copy-start.1
  0.0 2.9 %shard_map.91 = (s32[16,8]{1,0:T(8,128)}, s32[16,1,128]{2,1,0:T(1,128)}) custom-call(s32[64]{0:T(128)} %opening.1, s32[64]{0:T(128)} %bitcast.7, s32[64]{0:T(128)} %place.1), custom_call_target="tpu_custom_call" | custom-call | tf_op jit(solution)/shard_map/pallas_call | solution.py:537
  2.9 0.0 copy-start.3
  2.9 0.0 copy-start.4
  2.9 1.7 %reshape_squeeze.3 = bf16[512,2,2,2,128]{4,3,2,1,0:T(2,128)(2,1)S(1)} reshape(bf16[1,1,512,2,512]{4,3,2,1,0:T(2,128)(2,1)} %param.9) | data formatting | bytes 2097152 | tf_op jit(solution)/shard_map/reshape;squeeze | solution.py:549
  4.7 0.7 copy.10
  5.4 0.0 copy-done.3
  5.4 0.0 copy-done.4
  5.4 97.5 %shard_map.92 = (bf16[2,16,128,4,128]{4,3,2,1,0:T(4,128)(2,1)S(1)}, s32[16,1,128]{2,1,0:T(1,128)S(1)}) custom-call(s32[16,8]{1,0:T(8,128)S(1)} %copy-done.3, s32[16,1,128]{2,1,0:T(1,128)S(1)} %copy-done.4, bf16[2,512,4,128]{3,2,1,0:T(4,128)(2,1)S(1)} %bitcast.5), custom_call_target="tpu_custom_call" | custom-call | tf_op jit(solution)/shard_map/pallas_call | solution.py:554
  102.9 0.0 copy-done.2
  102.9 0.0 copy-done.1
  102.9 5.4 %shard_map.93.looked = f32[64,128]{1,0:T(8,128)S(1)} custom-call(s32[16,1,128]{2,1,0:T(1,128)S(1)} %get-tuple-element.11.labels, bf16[2,16,128,4,128]{4,3,2,1,0:T(4,128)(2,1)S(1)} %get-tuple-element.12.arrived, f32[2,128,128]{2,1,0:T(8,128)S(1)} %copy-done.1, f32[64,256]{1,0:T(8,128)S(1)} %copy-done.2), custom_call_target="tpu_custom_call" | custom-call | tf_op jit(solution)/shard_map/pallas_call | solution.py:583
  108.3 0.0 copy-start
  108.3 0.6 copy-done
  108.9 5.6 %shard_map.94 = f32[2,64,64]{2,1,0:T(8,128)} custom-call(f32[64,128]{1,0:T(8,128)} %copy-done, f32[128,64]{1,0:T(8,128)} %constant.12.clone.left, f32[128,128]{1,0:T(8,128)} %constant.13.clone.right, f32[128,128]{1,0:T(8,128)} %constant.14.clone.right_back), custom_call_target="tpu_custom_call" | custom-call | tf_op jit(solution)/shard_map/pallas_call | solution.py:595
  114.6 1.5 %copy.12 = f32[1,1,1,2,64,64]{5,4,3,2,1,0:T(8,128)} copy(f32[1,1,1,2,64,64]{5,4,3,2,1,0:T(8,128)} %bitcast.6) | data formatting | bytes 65536
Async XLA Ops:
  0.0 102.9 %copy-start.2 = (f32[64,256]{1,0:T(8,128)S(1)}, f32[64,256]{1,0:T(8,128)}, u32[]{:S(2)}) copy-start(f32[64,256]{1,0:T(8,128)} %constant.11.clone.gather) | copy-start | bytes 196612
  0.0 102.9 %copy-start.1 = (f32[2,128,128]{2,1,0:T(8,128)S(1)}, f32[2,128,128]{2,1,0:T(8,128)}, u32[]{:S(2)}) copy-start(f32[2,128,128]{2,1,0:T(8,128)} %constant.10.clone.spread) | copy-start | bytes 393220
  2.9 2.5 %copy-start.3 = (s32[16,8]{1,0:T(8,128)S(1)}, s32[16,8]{1,0:T(8,128)}, u32[]{:S(2)}) copy-start(s32[16,8]{1,0:T(8,128)} %get-tuple-element.9.starts) | copy-start | bytes 1540
  2.9 2.5 %copy-start.4 = (s32[16,1,128]{2,1,0:T(1,128)S(1)}, s32[16,1,128]{2,1,0:T(1,128)}, u32[]{:S(2)}) copy-start(s32[16,1,128]{2,1,0:T(1,128)} %get-tuple-element.10.labels) | copy-start | bytes 24580
  108.3 0.6 copy-start

commit v7 on v6

--- a/solution.py
+++ b/solution.py
@@ -313,6 +313,10 @@
                     for chunk in range(CHUNKS):
                         burst(part, pair, chunk).start()
 
+        for part in range(2):
+            for chunk in range(CHUNKS):
+                burst(part, 0, chunk).wait_send()
+
     mirror = level + right * (3 - 2 * level)
 
     def near(step, carry):
@@ -421,9 +425,6 @@
             return carry
 
         lax.fori_loop(0, 8, settle, 0)
-        for part in range(2):
-            for chunk in range(CHUNKS):
-                burst(part, 0, chunk).wait_send()
 
 
 def combine_kernel(allowance, labels, arrived, spread, gather, looked, total, count, prods):

time: 116 us -> 146 us (1.26)
  Pallas kernels: 111 us -> 141 us
    pallas_call x1, Pallas kernels: 97.5 us -> 127 us  [local_pair(): pl.pallas_call(functools.partial(exchange_kernel, allowance), out_shape=(...]
where the time goes in v7:
time: 146 us
  Pallas kernels  141 us (97%)
  local copies, waits for them, and re-layouts  4.57 us (3%)
    pallas_call x1, Pallas kernels, local_pair(): pl.pallas_call(functools.partial(exchange_kernel, allowance), out_shape=(...  127 us
    pallas_call x1, Pallas kernels, local_pair(): pl.pallas_call(filter_kernel, out_shape=jax.ShapeDtypeStruct((2, 64, 64),...  5.62 us
    pallas_call x1, Pallas kernels, local_pair(): pl.pallas_call(functools.partial(combine_kernel, allowance), out_shape=ja...  5.26 us

profile of v7, /device:TPU:3, one launch (start us, length us, event | category | flops | bytes accessed | tf_op | source)
XLA Modules:
  0.0 145.6 jit_solution(2134037487843699381)
XLA Ops:
  0.0 0.0 copy-start.2
  0.0 0.0 copy-start.1
  0.0 2.9 %shard_map.91 = (s32[16,8]{1,0:T(8,128)}, s32[16,1,128]{2,1,0:T(1,128)}) custom-call(s32[64]{0:T(128)} %opening.1, s32[64]{0:T(128)} %bitcast.7, s32[64]{0:T(128)} %place.1), custom_call_target="tpu_custom_call" | custom-call | tf_op jit(solution)/shard_map/pallas_call | solution.py:538
  2.9 0.0 copy-start.3
  2.9 0.0 copy-start.4
  2.9 1.7 %reshape_squeeze.3 = bf16[512,2,2,2,128]{4,3,2,1,0:T(2,128)(2,1)S(1)} reshape(bf16[1,1,512,2,512]{4,3,2,1,0:T(2,128)(2,1)} %param.9) | data formatting | bytes 2097152 | tf_op jit(solution)/shard_map/reshape;squeeze | solution.py:550
  4.7 0.7 copy.10
  5.4 0.0 copy-done.3
  5.4 0.0 copy-done.4
  5.4 127.1 %shard_map.92 = (bf16[2,16,128,4,128]{4,3,2,1,0:T(4,128)(2,1)S(1)}, s32[16,1,128]{2,1,0:T(1,128)S(1)}) custom-call(s32[16,8]{1,0:T(8,128)S(1)} %copy-done.3, s32[16,1,128]{2,1,0:T(1,128)S(1)} %copy-done.4, bf16[2,512,4,128]{3,2,1,0:T(4,128)(2,1)S(1)} %bitcast.5), custom_call_target="tpu_custom_call" | custom-call | tf_op jit(solution)/shard_map/pallas_call | solution.py:555
  132.6 0.0 copy-done.2
  132.6 0.0 copy-done.1
  132.6 5.3 %shard_map.93.looked = f32[64,128]{1,0:T(8,128)S(1)} custom-call(s32[16,1,128]{2,1,0:T(1,128)S(1)} %get-tuple-element.11.labels, bf16[2,16,128,4,128]{4,3,2,1,0:T(4,128)(2,1)S(1)} %get-tuple-element.12.arrived, f32[2,128,128]{2,1,0:T(8,128)S(1)} %copy-done.1, f32[64,256]{1,0:T(8,128)S(1)} %copy-done.2), custom_call_target="tpu_custom_call" | custom-call | tf_op jit(solution)/shard_map/pallas_call | solution.py:584
  137.9 0.0 copy-start
  137.9 0.6 copy-done
  138.5 5.6 %shard_map.94 = f32[2,64,64]{2,1,0:T(8,128)} custom-call(f32[64,128]{1,0:T(8,128)} %copy-done, f32[128,64]{1,0:T(8,128)} %constant.12.clone.left, f32[128,128]{1,0:T(8,128)} %constant.13.clone.right, f32[128,128]{1,0:T(8,128)} %constant.14.clone.right_back), custom_call_target="tpu_custom_call" | custom-call | tf_op jit(solution)/shard_map/pallas_call | solution.py:596
  144.1 1.5 %copy.12 = f32[1,1,1,2,64,64]{5,4,3,2,1,0:T(8,128)} copy(f32[1,1,1,2,64,64]{5,4,3,2,1,0:T(8,128)} %bitcast.6) | data formatting | bytes 65536
Async XLA Ops:
  0.0 132.6 %copy-start.2 = (f32[64,256]{1,0:T(8,128)S(1)}, f32[64,256]{1,0:T(8,128)}, u32[]{:S(2)}) copy-start(f32[64,256]{1,0:T(8,128)} %constant.11.clone.gather) | copy-start | bytes 196612
  0.0 132.6 %copy-start.1 = (f32[2,128,128]{2,1,0:T(8,128)S(1)}, f32[2,128,128]{2,1,0:T(8,128)}, u32[]{:S(2)}) copy-start(f32[2,128,128]{2,1,0:T(8,128)} %constant.10.clone.spread) | copy-start | bytes 393220
  2.9 2.5 %copy-start.3 = (s32[16,8]{1,0:T(8,128)S(1)}, s32[16,8]{1,0:T(8,128)}, u32[]{:S(2)}) copy-start(s32[16,8]{1,0:T(8,128)} %get-tuple-element.9.starts) | copy-start | bytes 1540
  2.9 2.5 %copy-start.4 = (s32[16,1,128]{2,1,0:T(1,128)S(1)}, s32[16,1,128]{2,1,0:T(1,128)}, u32[]{:S(2)}) copy-start(s32[16,1,128]{2,1,0:T(1,128)} %get-tuple-element.10.labels) | copy-start | bytes 24580
  137.9 0.6 copy-start
